TPU v7x, 256 devices: a whole 4x4x8 slice. The times are simulated.
256 devices in a mesh: grp: 2 (over x_hi), seq: 64 (over y, z, core), head: 2 (over x_lo).
Axes of the slice: x: 4 (x_hi: 2, x_lo: 2; x = x_hi * 2 + x_lo), y: 4, z: 8, core: 2. Of those that a mesh axis runs over, the one named last changes fastest.
Arguments:
- patches: bfloat16 [24576, 1280], P(('grp', 'seq')), parts along dimension 0, may hold values from -6 to 6
- ln_gain: float32 [1280], replicated, may hold values from 0.25 to 1.75
- ln_bias: float32 [1280], replicated, may hold values from -3 to 3
- qkv_weight: bfloat16 [1280, 3, 1280], P(None, None, 'head'), may hold values from -0.15625 to 0.15625
- proj_weight: bfloat16 [1280, 1280], P('head'), may hold values from -0.15625 to 0.15625
- proj_bias: float32 [1280], replicated, may hold values from -3 to 3
- merge_gain: float32 [1280], replicated, may hold values from 0.25 to 1.75
- merge_bias: float32 [1280], replicated, may hold values from -3 to 3
- visual_kv_weight: bfloat16 [5120, 2, 512], P(None, None, 'head'), may hold values from -0.078125 to 0.078125
- image_tokens: int32 [256], P('grp'), parts along dimension 0, may hold values from 2 to 47, as said below
- text_before: int32 [256], P('grp'), parts along dimension 0, may hold values from 0 to 8192, as said below
- text_order: int32 [16384], P(('grp', 'seq')), parts along dimension 0, may hold values from 0 to 8191, each once
- queries: bfloat16 [16384, 4096], P(('grp', 'seq'), 'head'), parts along dimension 0, may hold values from -44 to 44
- text_kv: bfloat16 [16384, 2, 512], P(('grp', 'seq'), None, 'head'), parts along dimension 0, may hold values from -4 to 4
Outputs:
- attended: bfloat16 [16384, 4096], P(('grp', 'seq'), 'head'), parts along dimension 0
- visual_kv: bfloat16 [6144, 2, 512], P(('grp', 'seq'), None, 'head'), parts along dimension 0
There are 2 independent parts, one for each index of `grp`. A program takes and returns all parts, laid end to end along the dimension named above; an argument that names none is the same for every part. Nothing has to cross between parts.
Inputs may be any that keep to these rules, and one draw needn't show every extreme that they name: `image_tokens`: they sum to 3072; each run of 48 visual tokens of one index of seq holds the last token of exactly two images (the last index: of one image and of the last image), so an image crosses every boundary between indices; the last image holds 47 tokens. `text_before`: non-decreasing. `text_order`: each number once.
All inputs are finite; a program needn't handle non-finite values.
Results may differ from a plain program's by a relative error of at most 0.0095.
Values may be sent and summed in bfloat16 or wider, within the bound.
A program may use at most 128 MiB of HBM per device.

v0:
```python
import math

import jax
import jax.numpy as jnp
from jax import lax
from jax.sharding import Mesh
from jax.sharding import PartitionSpec as P

VIT_HD = 80
HEAD_DIM = 128
GROUP = 8
SEQ = ("seq_0", "seq_1", "seq_2")
GRP_SEQ = ("grp", "seq_0", "seq_1", "seq_2")


epsilon = 1e-06
masked_score = -1e30


def extended(cells, sides, width):
    for axis, dim in sides:
        count = lax.axis_size(axis)
        ends = count - 1
        head = lax.slice_in_dim(cells, 0, width, axis=dim)
        tail = lax.slice_in_dim(cells, cells.shape[dim] - width, cells.shape[dim], axis=dim)
        cells = jnp.concatenate(
            [
                lax.ppermute(tail, axis, [(i, (i + 1) % count) for i in range(ends)]),
                cells,
                lax.ppermute(head, axis, [((i + 1) % count, i) for i in range(ends)]),
            ],
            axis=dim,
        )
    return cells


def sent_to_all(shard, axis):
    size = lax.axis_size(axis)
    return lax.all_to_all(
        jnp.broadcast_to(shard[None], (size, *shard.shape)), axis, 0, 0, tiled=True
    )


def of_everyone(shard, axis):
    return sent_to_all(shard, axis).astype(jnp.float32).sum(axis=0)


def whole_of(shard, axes, dim):
    for axis in reversed(axes):
        shard = lax.all_gather(shard, axis, axis=dim, tiled=True)
    return shard


def layer_norm(inputs, scale_gain, shift_bias):
    centre = jnp.mean(inputs, axis=-1, keepdims=True)
    centred = inputs - centre
    spread = jnp.mean(centred * centred, axis=-1, keepdims=True)
    return centred * lax.rsqrt(spread + epsilon) * scale_gain + shift_bias


def per_device(
    patches,
    ln_gain,
    ln_bias,
    qkv_weight,
    proj_weight,
    proj_bias,
    merge_gain,
    merge_bias,
    visual_kv_weight,
    image_tokens,
    text_before,
    text_order,
    queries,
    text_kv,
):
    seq_index = lax.axis_index(SEQ)
    patch_rows = patches.shape[0]
    model_width = patches.shape[1]
    merged_rows = patch_rows // 4
    head_cols = qkv_weight.shape[2]
    local_heads = head_cols // VIT_HD
    normed = layer_norm(patches.astype(jnp.float32), ln_gain, ln_bias).astype(jnp.bfloat16)
    projected = jnp.dot(
        normed, qkv_weight.reshape(model_width, 3 * head_cols), preferred_element_type=jnp.float32
    )
    projected = projected.astype(jnp.bfloat16).reshape(patch_rows, 3, head_cols)
    near_kv = extended(projected[:, 1:], ((SEQ, 0),), patch_rows)
    total_patches = patch_rows * lax.axis_size(SEQ)
    image_ends = 4 * jnp.cumsum(image_tokens)
    near_index = seq_index * patch_rows - patch_rows + jnp.arange(3 * patch_rows, dtype=jnp.int32)
    near_ids = jnp.sum((near_index[:, None] >= image_ends[None, :]).astype(jnp.int32), axis=1)
    near_ids = jnp.where((near_index >= 0) & (near_index < total_patches), near_ids, -1)
    own_ids = near_ids[patch_rows : 2 * patch_rows]
    queries_vit = projected[:, 0].reshape(patch_rows, local_heads, VIT_HD)
    near_keys = near_kv[:, 0].reshape(3 * patch_rows, local_heads, VIT_HD)
    near_values = near_kv[:, 1].reshape(3 * patch_rows, local_heads, VIT_HD)
    scores = jnp.einsum(
        "qhd,khd->hqk", queries_vit, near_keys, preferred_element_type=jnp.float32
    ) / math.sqrt(VIT_HD)
    allowed = own_ids[:, None] == near_ids[None, :]
    scores = jnp.where(allowed[None], scores, masked_score)
    weights = jax.nn.softmax(scores, axis=-1).astype(jnp.bfloat16)
    vit_mixed = jnp.einsum("hqk,khd->qhd", weights, near_values, preferred_element_type=jnp.float32)
    vit_mixed = vit_mixed.astype(jnp.bfloat16).reshape(patch_rows, head_cols)
    partial_value = jnp.dot(vit_mixed, proj_weight, preferred_element_type=jnp.float32)
    summed = of_everyone(partial_value.astype(jnp.bfloat16), "head").astype(jnp.float32)
    encoded = (patches.astype(jnp.float32) + summed + proj_bias).astype(jnp.bfloat16)
    merged = layer_norm(encoded.astype(jnp.float32), merge_gain, merge_bias).astype(jnp.bfloat16)
    merged = merged.reshape(merged_rows, 4 * model_width)
    visual_kv = jnp.dot(
        merged, visual_kv_weight.reshape(4 * model_width, -1), preferred_element_type=jnp.float32
    )
    visual_kv = visual_kv.astype(jnp.bfloat16).reshape(merged_rows, 2, -1)
    text_pos = text_order + jnp.sum(
        jnp.where(text_before[None, :] <= text_order[:, None], image_tokens[None, :], 0), axis=1
    )
    image_starts = jnp.cumsum(image_tokens) - image_tokens
    steps_before = text_before - jnp.concatenate([jnp.zeros((1,), jnp.int32), text_before[:-1]])
    visual_index = seq_index * merged_rows + jnp.arange(merged_rows, dtype=jnp.int32)
    vis_pos = visual_index + jnp.sum(
        jnp.where(image_starts[None, :] <= visual_index[:, None], steps_before[None, :], 0), axis=1
    )
    token_rows = queries.shape[0]
    llm_heads = text_kv.shape[2] // HEAD_DIM
    queries_llm = queries.reshape(token_rows, llm_heads, GROUP, HEAD_DIM)

    def key_block(block_state, block_part):
        running_max, running_sum, running_out = block_state
        block_kv, block_pos = block_part
        key_count = block_kv.shape[0]
        block_keys = block_kv[:, 0].reshape(key_count, llm_heads, HEAD_DIM)
        block_values = block_kv[:, 1].reshape(key_count, llm_heads, HEAD_DIM)
        block_scores = jnp.einsum(
            "qhgd,khd->qhgk", queries_llm, block_keys, preferred_element_type=jnp.float32
        ) / math.sqrt(HEAD_DIM)
        visible = (block_pos[None, :] <= text_pos[:, None])[:, None, None, :]
        block_scores = jnp.where(visible, block_scores, masked_score)
        new_max = jnp.maximum(running_max, jnp.max(block_scores, axis=-1))
        block_weights = jnp.where(visible, jnp.exp(block_scores - new_max[..., None]), 0.0)
        rescale = jnp.exp(running_max - new_max)
        running_sum = running_sum * rescale + jnp.sum(block_weights, axis=-1)
        running_out = running_out * rescale[..., None] + jnp.einsum(
            "qhgk,khd->qhgd",
            block_weights.astype(jnp.bfloat16),
            block_values,
            preferred_element_type=jnp.float32,
        )
        return ((new_max, running_sum, running_out), None)

    start_state = (
        jnp.full((token_rows, llm_heads, GROUP), masked_score, jnp.float32),
        jnp.zeros((token_rows, llm_heads, GROUP), jnp.float32),
        jnp.zeros((token_rows, llm_heads, GROUP, HEAD_DIM), jnp.float32),
    )
    state_now = start_state
    piece_kv = whole_of(
        jnp.concatenate([text_kv, visual_kv], axis=0), ("seq_2", "seq_1", "seq_0"), 0
    )
    piece_pos = whole_of(jnp.concatenate([text_pos, vis_pos]), ("seq_2", "seq_1", "seq_0"), 0)
    key_count = piece_pos.shape[0]
    block_rows = min(key_count, 1024)
    whole_blocks = key_count // block_rows
    stacked = (
        piece_kv.reshape((whole_blocks, block_rows) + piece_kv.shape[1:]),
        piece_pos.reshape(whole_blocks, block_rows),
    )
    state_now, unused = lax.scan(key_block, state_now, stacked)
    running_max, running_sum, running_out = state_now
    attended = running_out / running_sum[..., None]
    return (attended.astype(jnp.bfloat16).reshape(token_rows, -1), visual_kv)


def solution(mesh):
    split = Mesh(
        mesh.devices.reshape(mesh.shape["grp"], 4, 8, 2, mesh.shape["head"]),
        ("grp", "seq_0", "seq_1", "seq_2", "head"),
    )
    in_specs = (
        P(GRP_SEQ, None),
        P(),
        P(),
        P(None, None, "head"),
        P("head", None),
        P(),
        P(),
        P(),
        P(None, None, "head"),
        P("grp"),
        P("grp"),
        P(GRP_SEQ),
        P(GRP_SEQ, "head"),
        P(GRP_SEQ, None, "head"),
    )
    out_specs = (P(GRP_SEQ, "head"), P(GRP_SEQ, None, "head"))
    return jax.shard_map(
        per_device, mesh=split, in_specs=in_specs, out_specs=out_specs, check_vma=False
    )
```

profile of v0, /device:TPU:1, one launch (start us, length us, event | category | flops | bytes accessed | tf_op | source)
XLA Modules:
  0.0 322.7 jit_solution(2886636221892659058)
XLA Ops:
  9.8 8.2 %copy.51 = bf16[1280,3,640]{0,2,1:T(8,128)(2,1)} copy(bf16[1280,3,640]{2,0,1:T(8,128)(2,1)} %param.19) | data formatting | bytes 9830400 | tf_op args[3]
  18.1 4.2 %convolution_convert_fusion = bf16[192,1920]{1,0:T(8,128)(2,1)S(1)} fusion(bf16[1280,1920]{0,1:T(8,128)(2,1)} %bitcast.91, bf16[192,1280]{1,0:T(8,128)(2,1)S(1)} %copy-done.2, f32[1280]{0:T(1024)S(1)} %copy-done.15, f32[1280]{0:T(1024)S(1)} %copy-done.16, f32[192]{0:T(256)S(1)} %add_rsqrt_fusion.1, f32[192]{0:T(256)S(1)} %broadcast_multiply_fusion.1), kind=kOutput, calls=%fused_computation.25 | convolution fusion | flops 945561600 | bytes 6155776 | tf_op jit(solution)/shard_map/dot_general | solution.py:84
  23.1 5.1 %collective-permute-start.1 = (bf16[192,2,640]{2,1,0:T(2,128)(2,1)S(1)}, bf16[192,2,640]{2,1,0:T(2,128)(2,1)}, u32[]{:S(2)}, u32[]{:S(2)}) collective-permute-start(bf16[192,2,640]{2,1,0:T(2,128)(2,1)S(1)} %slice.34), channel_id=1, source_target_pairs={{2,0},{4,2},{6,4},{8,6},{10,8},{12,10},{14,12},{16,14},{18,16},{20... | collective-permute-start | bytes 1474568 | tf_op jit(solution)/shard_map/ppermute | solution.py:30
  35.9 6.7 %pad_maximum_fusion = bf16[576,2,640]{2,1,0:T(2,128)(2,1)S(1)} fusion(bf16[192,2,640]{2,1,0:T(2,128)(2,1)} %collective-permute-done.1, bf16[192,2,640]{2,1,0:T(2,128)(2,1)S(1)} %slice.34, bf16[192,2,640]{2,1,0:T(2,128)(2,1)} %collective-permute-done), kind=kLoop, calls=%fused_computation.32 | loop fusion | flops 1474560 | bytes 2949120 | tf_op jit(solution)/shard_map/concatenate | solution.py:26
  42.6 2.9 fusion.49
  45.6 4.2 %copy.54 = bf16[576,1,640]{0,2,1:T(8,128)(2,1)} copy(bf16[576,1,640]{2,1,0:T(2,128)(2,1)} %get-tuple-element.122) | data formatting | bytes 1474560 | tf_op jit(solution)/shard_map/slice | solution.py:96
  49.8 3.1 copy.52
  52.9 4.8 %fusion.50 = (f32[8,192]{1,0:T(8,128)S(1)}, f32[8,192,576]{2,1,0:T(8,128)}) fusion(pred[192,576]{1,0:T(8,128)(4,1)} %broadcast_compare_fusion.1, bf16[192,8,80]{0,2,1:T(8,128)(2,1)S(1)} %bitcast.99, bf16[576,8,80]{0,2,1:T(8,128)(2,1)} %bitcast.95), kind=kOutput, calls=%fused_computation.81 | convolution fusion | flops 145097280 | bytes 4638720 | tf_op jit(solution)/shard_map/sub | solution.py:103
  57.7 3.1 fusion.22
  62.4 3.6 %all-to-all-start = ((bf16[2,192,1280]{2,1,0:T(8,128)(2,1)}), bf16[2,192,1280]{2,1,0:T(8,128)(2,1)S(1)}, u32[]{:S(2)}, u32[]{:S(2)}) async-start(bf16[2,192,1280]{2,1,0:T(8,128)(2,1)} %broadcast_in_dim.111), calls=%async_computation | async-start | bytes 1966080 | tf_op jit(solution)/shard_map/all_to_all | solution.py:39
  66.3 5.7 %copy.69 = bf16[640,8,2,256]{3,1,2,0:T(8,128)(2,1)} copy(bf16[640,8,2,256]{3,2,1,0:T(2,128)(2,1)} %bitcast.90) | data formatting | bytes 10485760
  72.0 7.1 %all-to-all-done = bf16[2,192,1280]{2,1,0:T(8,128)(2,1)S(1)} async-done(((bf16[2,192,1280]{2,1,0:T(8,128)(2,1)}), bf16[2,192,1280]{2,1,0:T(8,128)(2,1)S(1)}, u32[]{:S(2)}, u32[]{:S(2)}) %all-to-all-start) | async-done | bytes 983072 | tf_op jit(solution)/shard_map/all_to_all | solution.py:39
  80.5 3.5 %convolution_convert_fusion.2 = bf16[48,512]{1,0:T(8,128)(2,1)S(1)} fusion(bf16[48,5120]{1,0:T(8,128)(2,1)S(1)} %reshape.169, bf16[5120,512]{1,0:T(8,128)(2,1)} %bitcast.88), kind=kOutput, calls=%fused_computation.43 | convolution fusion | flops 251682816 | bytes 5783552 | tf_op jit(solution)/shard_map/dot_general | solution.py:111
  84.1 11.4 %all_gather.21 = bf16[704,2,256]{2,0,1:T(8,128)(2,1)} all-gather(bf16[176,2,256]{2,0,1:T(8,128)(2,1)S(1)} %pad_maximum_fusion.1), channel_id=1, replica_groups=mesh['grp'=2,'seq_0'=4,'seq_1'=8,'seq_2'=2,'head'=2] {'seq_0'}, dimensions={0}, use_global_device_ids=true | all-gather | bytes 901120 | tf_op jit(solution)/shard_map/all_gather | solution.py:50
  95.6 74.7 %all-gather.4.cloned.1.call-done = bf16[5632,2,256]{2,0,1:T(8,128)(2,1)} async-done(((bf16[704,2,256]{2,0,1:T(8,128)(2,1)}), bf16[5632,2,256]{2,0,1:T(8,128)(2,1)}) %all-gather.4.cloned.1.call-update) | async-done | bytes 5767184 | tf_op jit(solution)/shard_map/all_gather | solution.py:50
  173.4 6.8 %all-reduce = s32[704]{0:T(1024)S(1)} all-reduce(s32[704]{0:T(1024)S(1)} %add_dynamic-update-slice_fusion), channel_id=1, replica_groups=mesh['grp'=2,'seq_0'=4,'seq_1'=8,'seq_2'=2,'head'=2] {'seq_0'}, use_global_device_ids=true, to_apply=%add | all-reduce | flops 704 | bytes 5632
  180.5 21.3 %all-reduce.1 = s32[5632]{0:T(1024)S(1)} all-reduce(s32[5632]{0:T(1024)S(1)} %dynamic-update-slice.1), channel_id=1, replica_groups=mesh['grp'=2,'seq_0'=4,'seq_1'=8,'seq_2'=2,'head'=2] {'seq_1'}, use_global_device_ids=true, to_apply=%add.1 | all-reduce | flops 5632 | bytes 45056
  201.9 11.3 %all-gather = s32[2,1,5632]{2,1,0:T(1,128)S(1)} all-gather(s32[1,1,5632]{2,1,0:T(1,128)S(1)} %reshape.181), channel_id=1, replica_groups=mesh['grp'=2,'seq_0'=4,'seq_1'=8,'seq_2'=2,'head'=2] {'seq_2'}, dimensions={0}, use_global_device_ids=true | all-gather | bytes 67584 | tf_op jit(solution)/shard_map/all_gather | solution.py:50
  214.6 98.8 %while.15 = (s32[]{:T(128)}, f32[128,2,8]{0,2,1:T(8,128)S(1)}, f32[128,2,8]{0,2,1:T(8,128)S(1)}, f32[128,2,8,128]{0,3,2,1:T(8,128)}, s32[11,1024]{1,0:T(8,128)S(...) while((s32[]{:T(128)}, f32[128,2,8]{0,2,1:T(8,128)S(1)}, ...), condition=%wide.region_14.15_spmd.clone, body=%wide.region_11.14_spmd.clone.sunk | while | flops 1101932544 | bytes 44184248 | solution.py:168
  220.2 2.3 fusion.81
  247.2 2.3 fusion.81
  265.1 2.3 fusion.81
  292.1 2.3 fusion.81
  301.0 2.3 fusion.81
  (253 shorter events, 106.4 us)
Async XLA Ops:
  7.2 53.6 %copy-start = (bf16[640,1280]{1,0:T(8,128)(2,1)S(1)}, bf16[640,1280]{1,0:T(8,128)(2,1)}, u32[]{:S(2)}) copy-start(bf16[640,1280]{1,0:T(8,128)(2,1)} %param.20) | copy-start | bytes 4915204
  9.8 8.3 %copy-start.2 = (bf16[192,1280]{1,0:T(8,128)(2,1)S(1)}, bf16[192,1280]{1,0:T(8,128)(2,1)}, u32[]{:S(2)}) copy-start(bf16[192,1280]{1,0:T(8,128)(2,1)} %param.16) | copy-start | bytes 1474564
  9.8 8.3 %copy-start.15 = (f32[1280]{0:T(1024)S(1)}, f32[1280]{0:T(1024)}, u32[]{:S(2)}) copy-start(f32[1280]{0:T(1024)} %param.18) | copy-start | bytes 15364
  9.8 8.3 %copy-start.16 = (f32[1280]{0:T(1024)S(1)}, f32[1280]{0:T(1024)}, u32[]{:S(2)}) copy-start(f32[1280]{0:T(1024)} %param.17) | copy-start | bytes 15364
  18.1 12.1 %copy-start.12 = (s32[128]{0:T(128)S(1)}, s32[128]{0:T(128)}, u32[]{:S(2)}) copy-start(s32[128]{0:T(128)} %param.25) | copy-start | bytes 1540
  18.1 12.5 %copy-start.13 = (s32[128]{0:T(128)S(1)}, s32[128]{0:T(128)}, u32[]{:S(2)}) copy-start(s32[128]{0:T(128)} %param.26) | copy-start | bytes 1540
  23.1 11.5 %collective-permute-start.1 = (bf16[192,2,640]{2,1,0:T(2,128)(2,1)S(1)}, bf16[192,2,640]{2,1,0:T(2,128)(2,1)}, u32[]{:S(2)}, u32[]{:S(2)}) collective-permute-start(bf16[192,2,640]{2,1,0:T(2,128)(2,1)S(1)} %slice.34), channel_id=1, source_target_pairs={{2,0},{4,2},{6,4},{8,6},{10,8},{12,10},{14,12},{16,14},{18,16},{20... | collective-permute-start | bytes 1474568 | tf_op jit(solution)/shard_map/ppermute | solution.py:30
  28.2 7.7 %collective-permute-start = (bf16[192,2,640]{2,1,0:T(2,128)(2,1)S(1)}, bf16[192,2,640]{2,1,0:T(2,128)(2,1)}, u32[]{:S(2)}, u32[]{:S(2)}) collective-permute-start(bf16[192,2,640]{2,1,0:T(2,128)(2,1)S(1)} %slice.34), channel_id=1, source_target_pairs={{0,2},{2,4},{4,6},{6,8},{8,10},{10,12},{12,14},{14,16},{16,18},{18... | collective-permute-start | bytes 1474568 | tf_op jit(solution)/shard_map/ppermute | solution.py:28
  52.9 4.8 %copy-start.6 = (bf16[576,1,640]{0,2,1:T(8,128)(2,1)S(1)}, bf16[576,1,640]{0,2,1:T(8,128)(2,1)}, u32[]{:S(2)}) copy-start(bf16[576,1,640]{0,2,1:T(8,128)(2,1)} %copy.52) | copy-start | bytes 2211844
  60.7 5.5 %copy-start.8 = (bf16[128,2,256]{2,1,0:T(2,128)(2,1)S(1)}, bf16[128,2,256]{2,1,0:T(2,128)(2,1)}, u32[]{:S(2)}) copy-start(bf16[128,2,256]{2,1,0:T(2,128)(2,1)} %param.29) | copy-start | bytes 393220
  62.4 16.7 %all-to-all-start = ((bf16[2,192,1280]{2,1,0:T(8,128)(2,1)}), bf16[2,192,1280]{2,1,0:T(8,128)(2,1)S(1)}, u32[]{:S(2)}, u32[]{:S(2)}) async-start(bf16[2,192,1280]{2,1,0:T(8,128)(2,1)} %broadcast_in_dim.111), calls=%async_computation | async-start | bytes 1966080 | tf_op jit(solution)/shard_map/all_to_all | solution.py:39
  66.0 104.3 %all-gather.4.cloned.1.call-start = ((), (), s32[]{:S(2)}) async-start(), calls=%async_computation.1 | async-start | bytes 6488064 | tf_op jit(solution)/shard_map/all_gather | solution.py:50
  66.2 13.0 %copy-start.3 = (bf16[192,1280]{1,0:T(8,128)(2,1)S(1)}, bf16[192,1280]{1,0:T(8,128)(2,1)}, u32[]{:S(2)}) copy-start(bf16[192,1280]{1,0:T(8,128)(2,1)} %param.16) | copy-start | bytes 1474564
  66.2 13.0 %copy-start.9 = (f32[1280]{0:T(1024)S(1)}, f32[1280]{0:T(1024)}, u32[]{:S(2)}) copy-start(f32[1280]{0:T(1024)} %param.21) | copy-start | bytes 15364
  66.2 13.6 %copy-start.10 = (f32[1280]{0:T(1024)S(1)}, f32[1280]{0:T(1024)}, u32[]{:S(2)}) copy-start(f32[1280]{0:T(1024)} %param.23) | copy-start | bytes 15364
  66.3 13.6 %copy-start.11 = (f32[1280]{0:T(1024)S(1)}, f32[1280]{0:T(1024)}, u32[]{:S(2)}) copy-start(f32[1280]{0:T(1024)} %param.22) | copy-start | bytes 15364
  84.0 86.3 %copy-start.18 = (u32[256]{0:T(256)S(1)}, u32[256]{0:T(256)}, u32[]{:S(2)}) copy-start(u32[256]{0:T(256)} %constant.87) | copy-start | bytes 3076
  84.0 87.0 %copy-start.17 = (u32[256]{0:T(256)S(1)}, u32[256]{0:T(256)}, u32[]{:S(2)}) copy-start(u32[256]{0:T(256)} %constant.82) | copy-start | bytes 3076
  84.0 87.6 %copy-start.14 = (s32[128]{0:T(128)S(1)}, s32[128]{0:T(128)}, u32[]{:S(2)}) copy-start(s32[128]{0:T(128)} %param.27) | copy-start | bytes 1540
  84.0 129.3 %copy-start.7 = (bf16[128,2048]{1,0:T(8,128)(2,1)S(1)}, bf16[128,2048]{1,0:T(8,128)(2,1)}, u32[]{:S(2)}) copy-start(bf16[128,2048]{1,0:T(8,128)(2,1)} %param.28) | copy-start | bytes 1572868
  95.6 119.0 %all-gather.6.cloned.1.call-start = ((), (), s32[]{:S(2)}) async-start(), calls=%async_computation.2 | async-start | bytes 17301504 | tf_op jit(solution)/shard_map/all_gather | solution.py:50
  218.2 2.1 copy-start.4
  227.1 2.1 copy-start.4
  313.3 2.5 copy-start.1
  (20 other events, 29.3 us)
Sparse Core Ops, SparseCore 0:
  95.7 74.5 all-gather.3
  172.1 27.8 all-gather.5
where the time goes:
time: 324 us; the launch traced here: 323 us
  waiting for transfers between devices  83.3 us (26%)
  local copies, waits for them, and re-layouts  64.8 us (20%)
  matrix products  57.6 us (18%)
  blocking collectives  50.9 us (16%)
  other arithmetic  38.3 us (12%)
  between operations  15.8 us (5%)
  starting transfers between devices  10.9 us (3%)
    all_gather x2, waiting for transfers between devices, whole_of(): shard = lax.all_gather(shard, axis, axis=dim, tiled=True)  74.7 us
    unnamed x2, blocking collectives  28.2 us
    dot_general x11, matrix products, key_block(): jnp.einsum('qhgk,khd->qhgd', block_weights.astype(jnp.bfloat16), block_va...  25.5 us
    all_gather x2, blocking collectives, whole_of(): shard = lax.all_gather(shard, axis, axis=dim, tiled=True)  22.7 us
    reduce_sum x11, other arithmetic, key_block(): running_sum = running_sum * rescale + jnp.sum(block_weights, axis=-1)  22 us
    dynamic_slice x33, local copies, waits for them, and re-layouts, per_device(): state_now, unused = lax.scan(key_block, state_now, stacked)  20.3 us
    unnamed x45, local copies, waits for them, and re-layouts  16.2 us
    dot_general x11, matrix products, key_block(): jnp.einsum('qhgd,khd->qhgk', queries_llm, block_keys, preferred_element_t...  16 us
  transfers between devices with their start and end apart: 5, of which 4 were waited for; matrix products, arithmetic and copies ran while one was open for 4% of the time, Pallas kernels for 0%

commit v1 on v0

--- a/solution.py
+++ b/solution.py
@@ -1,16 +1,310 @@
+import functools
+import heapq
 import math
 
 import jax
 import jax.numpy as jnp
 from jax import lax
+from jax.experimental import pallas as pl
+from jax.experimental.pallas import tpu as pltpu
 from jax.sharding import Mesh
 from jax.sharding import PartitionSpec as P
+
+MESH = pl.DeviceIdType.MESH
+
 
 VIT_HD = 80
 HEAD_DIM = 128
 GROUP = 8
 SEQ = ("seq_0", "seq_1", "seq_2")
 GRP_SEQ = ("grp", "seq_0", "seq_1", "seq_2")
+
+
+NEG = -1e30
+C=math.log2(math.e)/math.sqrt(128)
+G=8; D=128
+BIG=2**30
+
+def attend_kernel(q_ref, kvt_ref, kvv_ref, qpos_ref, kp_ref, perm_ref, out_ref,
+                  kbuf, vbuf, s_sc, x_sc, p_sc, a_sc, o_sc, m_sc, l_sc, srt_sc, sem, *, TQ, NT, NV):
+    R=G*TQ
+    nq=128//TQ
+    KB=1024
+    S=kvt_ref.shape[0]
+    RB=KB//S
+    def copies(h,b):
+        out=[]
+        for j,buf in ((0,kbuf),(1,vbuf)):
+            c=j*256+h*D
+            if b<NT:
+                src=kvt_ref.at[:,b*RB:(b+1)*RB,c:c+D]
+                dst=buf.at[h,b]
+            else:
+                src=kvv_ref.at[b-NT,:,:,c:c+D]
+                dst=buf.at[h,b]
+            out.append(pltpu.make_async_copy(src,dst,sem.at[h,b]))
+        return out
+    for h in range(2):
+        for b in range(NT+NV):
+            for c in copies(h,b): c.start()
+    kmin=jnp.min(kp_ref[...],axis=1,keepdims=True)
+    tmin=kmin[0:NT]; vmin=kmin[NT:NT+NV]
+    for h in range(2):
+        for b in range(NT+NV):
+            for c in copies(h,b): c.wait()
+        for i in range(nq):
+            qp=qpos_ref[i*TQ:(i+1)*TQ,0:1]
+            qhi=jnp.max(qp,axis=0,keepdims=True)
+            nt=jnp.sum((tmin<=qhi).astype(jnp.int32))
+            nv=jnp.sum((vmin<=qhi).astype(jnp.int32))
+            n=nt+nv
+            q=jnp.concatenate([q_ref[i*TQ:(i+1)*TQ,(h*G+g)*D:(h*G+g+1)*D] for g in range(G)],axis=0)
+            def blk(j):
+                return jnp.minimum(jnp.where(j<nt,j,j-nt+NT),NT+NV-1)
+            def pblk(j):
+                return jnp.where(j<n,blk(j),NT+NV)
+            def qk(j,t):
+                k=kbuf[h,blk(j)].reshape(KB,D)
+                s=lax.dot_general(q,k,(((1,),(1,)),((),())),preferred_element_type=jnp.float32)
+                bias=jnp.where(kp_ref[pl.ds(pblk(j),1),:]<=qp,0.0,NEG)
+                s=s+jnp.concatenate([bias]*G,axis=0)
+                s_sc[t]=s
+                x=s[:,0:128]
+                for c in range(1,KB//128): x=jnp.maximum(x,s[:,c*128:(c+1)*128])
+                x_sc[t]=x
+            def soft(t):
+                m_old=m_sc[:,0:1]
+                m_new=jnp.maximum(m_old,jnp.max(x_sc[t],axis=1,keepdims=True))
+                mc=m_new*C
+                p=jnp.exp2(s_sc[t]*C-mc)
+                a=jnp.exp2(m_old*C-mc)
+                l=p[:,0:128]
+                for c in range(1,KB//128): l=l+p[:,c*128:(c+1)*128]
+                l_sc[...]=l_sc[...]*a+l
+                p_sc[t]=p.astype(jnp.bfloat16)
+                a_sc[t]=jnp.broadcast_to(a,(R,128))
+                m_sc[...]=jnp.broadcast_to(m_new,m_sc.shape)
+            def pv(j,t):
+                v=vbuf[h,blk(jnp.maximum(j,0))].reshape(KB,D)
+                o_sc[...]=o_sc[...]*a_sc[t]+jnp.dot(p_sc[t],v,preferred_element_type=jnp.float32)
+            m_sc[...]=jnp.full_like(m_sc,NEG)
+            l_sc[...]=jnp.zeros_like(l_sc)
+            o_sc[...]=jnp.zeros_like(o_sc)
+            p_sc[1]=jnp.zeros_like(p_sc[1])
+            a_sc[1]=jnp.zeros_like(a_sc[1])
+            qk(0,0)
+            @pl.loop(0,(n+1)//2)
+            def _(jj):
+                j=jj*2
+                pv(j-1,1); qk(j+1,1); soft(0)
+                pv(j,0); qk(j+2,0); soft(1)
+            pv(((n+1)//2)*2-1,1)
+            o=(o_sc[...]/jnp.sum(l_sc[...],axis=1,keepdims=True)).astype(jnp.bfloat16)
+            for g in range(G):
+                srt_sc[i*TQ:(i+1)*TQ,g*D:(g+1)*D]=o[g*TQ:(g+1)*TQ]
+        out_ref[:,h*1024:(h+1)*1024]=jnp.dot(perm_ref[...],srt_sc[...],preferred_element_type=jnp.float32).astype(jnp.bfloat16)
+
+def attend(q,kvt,kvv,qpos,kp,perm):
+    S=kvt.shape[0]; V=kvv.shape[0]*kvv.shape[1]
+    KB=1024; RB=KB//S; NT=S*128//KB; NV=V//KB
+    kvv4=kvv.reshape(NV,S,RB,512)
+    TQ=32
+    R=G*TQ
+    vm=lambda: pl.BlockSpec(memory_space=pltpu.VMEM)
+    hb=lambda: pl.BlockSpec(memory_space=pl.ANY)
+    return pl.pallas_call(
+        functools.partial(attend_kernel,TQ=TQ,NT=NT,NV=NV),
+        in_specs=[vm(),hb(),hb(),vm(),vm(),vm()],
+        out_specs=vm(),
+        out_shape=jax.ShapeDtypeStruct((128,2048),jnp.bfloat16),
+        scratch_shapes=[pltpu.VMEM((2,NT+NV,S,RB,D),jnp.bfloat16),pltpu.VMEM((2,NT+NV,S,RB,D),jnp.bfloat16),
+          pltpu.VMEM((2,R,KB),jnp.float32),pltpu.VMEM((2,R,128),jnp.float32),pltpu.VMEM((2,R,KB),jnp.bfloat16),pltpu.VMEM((2,R,128),jnp.float32),
+          pltpu.VMEM((R,128),jnp.float32),pltpu.VMEM((R,128),jnp.float32),pltpu.VMEM((R,128),jnp.float32),pltpu.VMEM((128,1024),jnp.bfloat16),
+          pltpu.SemaphoreType.DMA((2,NT+NV))],
+        compiler_params=pltpu.CompilerParams(vmem_limit_bytes=60<<20),
+        name="attend",
+    )(q,kvt,kvv4,qpos,kp,perm)
+
+
+def ring_plan(na, nb):
+    free = {}
+    heap = []
+    count = [0]
+    def send(axis, way, a, b, part, at):
+        start = max(at, free.get((axis, way), 0.0))
+        end = start + (1.0 if part == 0 else 0.5)
+        free[(axis, way)] = end
+        count[0] += 1
+        heapq.heappush(heap, (end + 0.9, count[0], axis, way, a, b, part))
+    def spread(axis, size, way, off, at, a, b):
+        nxt = off + 1
+        if nxt < size // 2:
+            part = 0
+        elif nxt == size // 2:
+            part = 1 if way == 1 else 2
+        else:
+            return None
+        return part
+    def go(axis, size, way, off, at, a, b):
+        part = spread(axis, size, way, off, at, a, b)
+        if part is not None:
+            na_, nb_ = (a + way, b) if axis == "a" else (a, b + way)
+            send(axis, way, na_, nb_, part, at)
+    for way in (1, -1):
+        go("a", na, way, 0, 0.0, 0, 0)
+    for way in (1, -1):
+        go("b", nb, way, 0, 0.0, 0, 0)
+    order = []
+    halves = {}
+    while heap:
+        at, _, axis, way, a, b, part = heapq.heappop(heap)
+        order.append((axis, way, a, b, part))
+        if axis == "a":
+            if part == 0:
+                go("a", na, way, abs(a), at, a, b)
+                for w in (1, -1):
+                    go("b", nb, w, 0, at, a, b)
+            else:
+                key = abs(a)
+                halves[("a", key, b)] = halves.get(("a", key, b), 0) + 1
+                if halves[("a", key, b)] == 2:
+                    for w in (1, -1):
+                        go("b", nb, w, 0, at, na // 2, b)
+        else:
+            if part == 0:
+                go("b", nb, way, abs(b), at, a, b)
+    return order
+
+class Gather:
+    def __init__(self, own, out, rows, cut, send_sem, recv_sem, ny=4, nz=8):
+        self.own, self.out, self.rows, self.cut = own, out, rows, cut
+        self.send_sem, self.recv_sem = send_sem, recv_sem
+        self.ny, self.nz = ny, nz
+        self.y, self.z, self.c = lax.axis_index("seq_0"), lax.axis_index("seq_1"), lax.axis_index("seq_2")
+        self.sent = []
+        self.plans = [ring_plan(nz, ny), ring_plan(ny, nz)]
+    def sid(self, c, a, b):
+        dz, dy = (a, b) if c == 0 else (b, a)
+        y = lax.rem(self.y - dy + self.ny, self.ny)
+        z = lax.rem(self.z - dz + self.nz, self.nz)
+        return (y * self.nz + z) * 2 + c
+    def part(self, ref, part):
+        if part == 0: return ref
+        return ref.at[0:self.cut] if part == 1 else ref.at[self.cut:self.rows]
+    def desc(self, src, s, part, n, dev):
+        return pltpu.make_async_remote_copy(
+            src_ref=self.part(src, part), dst_ref=self.part(self.out.at[s], part),
+            send_sem=self.send_sem.at[n], recv_sem=self.recv_sem.at[s, 1 if part == 2 else 0],
+            device_id=dev, device_id_type=MESH)
+    def neighbour(self, c, axis, way):
+        along_z = (axis == "a") == (c == 0)
+        if along_z:
+            return {"seq_1": lax.rem(self.z + way + self.nz, self.nz)}
+        return {"seq_0": lax.rem(self.y + way + self.ny, self.ny)}
+    def start(self, c, src, s, part, dev):
+        d = self.desc(src, s, part, len(self.sent), dev)
+        d.start()
+        self.sent.append(d)
+    def wait(self, s, part):
+        self.desc(self.out.at[s], s, part, 0, {"seq_2": 1 - self.c}).wait_recv()
+    def to_partner(self, src, s):
+        self.start(None, src, s, 0, {"seq_2": 1 - self.c})
+    def begin(self, c):
+        self.sent = []
+        s = self.sid(c, 0, 0)
+        for axis in ("a", "b"):
+            for way in (1, -1):
+                self.start(c, self.own, s, 0, self.neighbour(c, axis, way))
+        self.to_partner(self.own, s)
+    def events(self, c):
+        na, nb = (self.nz, self.ny) if c == 0 else (self.ny, self.nz)
+        steps = []
+        halves = {}
+        def step(axis, way, a, b, part):
+            s = self.sid(c, a, b)
+            self.wait(s, part)
+            src = self.out.at[s]
+            size = na if axis == "a" else nb
+            off = abs(a) if axis == "a" else abs(b)
+            if part == 0:
+                nxt = off + 1
+                if nxt < size // 2: p = 0
+                else: p = 1 if way == 1 else 2
+                self.start(c, src, s, p, self.neighbour(c, axis, way))
+                done = True
+            else:
+                key = (axis, off, abs(a) if abs(a)*2==na else a)
+                halves[key] = halves.get(key, 0) + 1
+                done = halves[key] == 2
+            if done:
+                if axis == "a":
+                    for w in (1, -1):
+                        self.start(c, src, s, 0, self.neighbour(c, "b", w))
+                self.to_partner(src, s)
+        for e in self.plans[c]:
+            steps.append(functools.partial(step, *e))
+        return steps
+    def finish(self, c):
+        na, nb = (self.nz, self.ny) if c == 0 else (self.ny, self.nz)
+        for a in range(na):
+            for b in range(nb):
+                self.wait(self.sid(1 - c, a, b) if False else self.other(c, a, b), 0)
+        for d in self.sent:
+            d.wait_send()
+    def other(self, c, a, b):
+        return self.sid(1 - c, *((b, a)))
+
+def barrier(peers_fn):
+    sem = pltpu.get_barrier_semaphore()
+    y, z, c = lax.axis_index("seq_0"), lax.axis_index("seq_1"), lax.axis_index("seq_2")
+    n = 0
+    for dev in peers_fn(y, z, c):
+        pl.semaphore_signal(sem, inc=1, device_id=dev, device_id_type=MESH); n += 1
+    pl.semaphore_wait(sem, n)
+
+def near(y, z, c, ny=4, nz=8):
+    return [{"seq_0": lax.rem(y + 1, ny)}, {"seq_0": lax.rem(y + ny - 1, ny)},
+            {"seq_1": lax.rem(z + 1, nz)}, {"seq_1": lax.rem(z + nz - 1, nz)}, {"seq_2": 1 - c}]
+
+
+def gather_kernel(text_ref, vis_ref, text_out, vis_out, ts, tr, vs, vr, loc_sem, *, ny, nz):
+    barrier(functools.partial(near, ny=ny, nz=nz))
+    core = lax.axis_index("seq_2")
+    me = (lax.axis_index("seq_0") * nz + lax.axis_index("seq_1")) * 2 + core
+    locs = [pltpu.make_async_copy(text_ref, text_out.at[me], loc_sem.at[0]),
+            pltpu.make_async_copy(vis_ref, vis_out.at[me], loc_sem.at[1])]
+    for loc in locs:
+        loc.start()
+    for c in (0, 1):
+        @pl.when(core == c)
+        def _():
+            v = Gather(vis_ref, vis_out, vis_ref.shape[0], vis_ref.shape[0] // 2, vs, vr, ny, nz)
+            t = Gather(text_ref, text_out, text_ref.shape[0], 64, ts, tr, ny, nz)
+            v.begin(c)
+            t.begin(c)
+            for a, b in zip(v.events(c), t.events(c)):
+                a()
+                b()
+            v.finish(c)
+            t.finish(c)
+    for loc in locs:
+        loc.wait()
+
+
+def gather(text, vis, ny, nz):
+    n = ny * nz * 2
+    any_space = pl.BlockSpec(memory_space=pl.ANY)
+    in_vmem = pl.BlockSpec(memory_space=pltpu.VMEM)
+    dma = pltpu.SemaphoreType.DMA
+    return pl.pallas_call(
+        functools.partial(gather_kernel, ny=ny, nz=nz),
+        in_specs=[in_vmem, in_vmem],
+        out_specs=[any_space, any_space],
+        out_shape=[jax.ShapeDtypeStruct((n, *x.shape), x.dtype) for x in (text, vis)],
+        scratch_shapes=[dma((2 * n + 16,)), dma((n, 2)), dma((2 * n + 16,)), dma((n, 2)), dma((2,))],
+        compiler_params=pltpu.CompilerParams(collective_id=1, has_side_effects=True),
+        name="gather",
+    )(text, vis)
 
 
 epsilon = 1e-06
@@ -43,12 +337,6 @@
 
 def of_everyone(shard, axis):
     return sent_to_all(shard, axis).astype(jnp.float32).sum(axis=0)
-
-
-def whole_of(shard, axes, dim):
-    for axis in reversed(axes):
-        shard = lax.all_gather(shard, axis, axis=dim, tiled=True)
-    return shard
 
 
 def layer_norm(inputs, scale_gain, shift_bias):
@@ -117,58 +405,31 @@
     )
     image_starts = jnp.cumsum(image_tokens) - image_tokens
     steps_before = text_before - jnp.concatenate([jnp.zeros((1,), jnp.int32), text_before[:-1]])
-    visual_index = seq_index * merged_rows + jnp.arange(merged_rows, dtype=jnp.int32)
-    vis_pos = visual_index + jnp.sum(
+
+    tokens = queries.shape[0]
+    ny, nz = lax.axis_size("seq_0"), lax.axis_size("seq_1")
+    rank = jnp.sum((text_order[None, :] < text_order[:, None]).astype(jnp.int32), axis=1)
+    hot = (rank[None, :] == jnp.arange(tokens, dtype=jnp.int32)[:, None]).astype(jnp.bfloat16)
+    q = jnp.dot(hot, queries, preferred_element_type=jnp.float32).astype(jnp.bfloat16)
+    places = jnp.stack([text_pos // 128, text_pos % 128]).astype(jnp.bfloat16)
+    places = lax.dot_general(places, hot, (((1,), (1,)), ((), ())), preferred_element_type=jnp.float32)
+    kv = jnp.dot(hot, text_kv.reshape(tokens, -1), preferred_element_type=jnp.float32).astype(jnp.bfloat16)
+    places_rows = jnp.pad(places.astype(jnp.bfloat16), ((0, 6), (0, kv.shape[1] - tokens)))
+    all_text, all_vis = gather(jnp.concatenate([kv, places_rows], axis=0), visual_kv.reshape(merged_rows, -1), ny, nz)
+    key_pos = all_text[:, tokens : tokens + 2, :tokens].astype(jnp.int32)
+    key_pos = key_pos[:, 0] * 128 + key_pos[:, 1]
+    sources = key_pos.shape[0]
+    blocks = sources * tokens // 1024
+    key_pos = key_pos.reshape(sources, blocks, tokens // blocks).transpose(1, 0, 2).reshape(blocks, 1024)
+    visual_index = jnp.arange(sources * merged_rows, dtype=jnp.int32)
+    all_vis_pos = visual_index + jnp.sum(
         jnp.where(image_starts[None, :] <= visual_index[:, None], steps_before[None, :], 0), axis=1
     )
-    token_rows = queries.shape[0]
-    llm_heads = text_kv.shape[2] // HEAD_DIM
-    queries_llm = queries.reshape(token_rows, llm_heads, GROUP, HEAD_DIM)
-
-    def key_block(block_state, block_part):
-        running_max, running_sum, running_out = block_state
-        block_kv, block_pos = block_part
-        key_count = block_kv.shape[0]
-        block_keys = block_kv[:, 0].reshape(key_count, llm_heads, HEAD_DIM)
-        block_values = block_kv[:, 1].reshape(key_count, llm_heads, HEAD_DIM)
-        block_scores = jnp.einsum(
-            "qhgd,khd->qhgk", queries_llm, block_keys, preferred_element_type=jnp.float32
-        ) / math.sqrt(HEAD_DIM)
-        visible = (block_pos[None, :] <= text_pos[:, None])[:, None, None, :]
-        block_scores = jnp.where(visible, block_scores, masked_score)
-        new_max = jnp.maximum(running_max, jnp.max(block_scores, axis=-1))
-        block_weights = jnp.where(visible, jnp.exp(block_scores - new_max[..., None]), 0.0)
-        rescale = jnp.exp(running_max - new_max)
-        running_sum = running_sum * rescale + jnp.sum(block_weights, axis=-1)
-        running_out = running_out * rescale[..., None] + jnp.einsum(
-            "qhgk,khd->qhgd",
-            block_weights.astype(jnp.bfloat16),
-            block_values,
-            preferred_element_type=jnp.float32,
-        )
-        return ((new_max, running_sum, running_out), None)
-
-    start_state = (
-        jnp.full((token_rows, llm_heads, GROUP), masked_score, jnp.float32),
-        jnp.zeros((token_rows, llm_heads, GROUP), jnp.float32),
-        jnp.zeros((token_rows, llm_heads, GROUP, HEAD_DIM), jnp.float32),
-    )
-    state_now = start_state
-    piece_kv = whole_of(
-        jnp.concatenate([text_kv, visual_kv], axis=0), ("seq_2", "seq_1", "seq_0"), 0
-    )
-    piece_pos = whole_of(jnp.concatenate([text_pos, vis_pos]), ("seq_2", "seq_1", "seq_0"), 0)
-    key_count = piece_pos.shape[0]
-    block_rows = min(key_count, 1024)
-    whole_blocks = key_count // block_rows
-    stacked = (
-        piece_kv.reshape((whole_blocks, block_rows) + piece_kv.shape[1:]),
-        piece_pos.reshape(whole_blocks, block_rows),
-    )
-    state_now, unused = lax.scan(key_block, state_now, stacked)
-    running_max, running_sum, running_out = state_now
-    attended = running_out / running_sum[..., None]
-    return (attended.astype(jnp.bfloat16).reshape(token_rows, -1), visual_kv)
+    kp = jnp.concatenate([key_pos, all_vis_pos.reshape(-1, 1024), jnp.full((1, 1024), BIG, jnp.int32)], axis=0)
+    places = places.astype(jnp.int32)
+    q_pos = (places[0] * 128 + places[1])[:, None]
+    attended = attend(q, all_text, all_vis, q_pos, kp, hot.T)
+    return (attended, visual_kv)
 
 
 def solution(mesh):

time: 324 us -> 179 us (0.55)
  Pallas kernels: 0 us -> 97.2 us
  waiting for transfers between devices: 83.3 us -> 3.53 us
  blocking collectives: 50.9 us -> 0 us
  matrix products: 57.6 us -> 17.6 us
  local copies, waits for them, and re-layouts: 64.8 us -> 31.6 us
  other arithmetic: 38.3 us -> 14.8 us
  between operations: 15.8 us -> 1.21 us
    pallas_call x0 -> x2, Pallas kernels: none -> 97.2 us  [the longest x1 53.9 us: gather(): pl.pallas_call(functools.partial(gather_kernel, ny=ny, nz=nz), in_specs=[...]
    all_gather x2 -> x0, waiting for transfers between devices: 74.7 us -> none  [whole_of(): shard = lax.all_gather(shard, axis, axis=dim, tiled=True)]
    dot_general x22 -> x3, matrix products: 41.5 us -> 1.41 us  [the longest x1 1.1 us: per_device(): jnp.dot(hot, queries, preferred_element_type=jnp.float32)]
    unnamed x2 -> x0, blocking collectives: 28.2 us -> none
    all_gather x2 -> x0, blocking collectives: 22.7 us -> none  [whole_of(): shard = lax.all_gather(shard, axis, axis=dim, tiled=True)]
    reduce_sum x11 -> x0, other arithmetic: 22 us -> none  [key_block(): running_sum = running_sum * rescale + jnp.sum(block_weights, axis=-1)]
    dynamic_slice x33 -> x0, local copies, waits for them, and re-layouts: 20.3 us -> none  [per_device(): state_now, unused = lax.scan(key_block, state_now, stacked)]
    while x55 -> x0, local copies, waits for them, and re-layouts: 10.7 us -> none
  transfers between devices with their start and end apart: 5 -> 3, of which waited for: 4 -> 2; matrix products, arithmetic and copies ran while one was open for 4% -> 8% of each run, Pallas kernels for 0% -> 0%
where the time goes in v1:
time: 179 us; the launch traced here: 177 us
  Pallas kernels  97.2 us (54%)
  local copies, waits for them, and re-layouts  31.6 us (18%)
  matrix products  17.6 us (10%)
  other arithmetic  14.8 us (8%)
  starting transfers between devices  10.8 us (6%)
  waiting for transfers between devices  3.53 us (2%)
    pallas_call x1, Pallas kernels, gather(): pl.pallas_call(functools.partial(gather_kernel, ny=ny, nz=nz), in_specs=[...  53.9 us
    pallas_call x1, Pallas kernels, attend(): pl.pallas_call(functools.partial(attend_kernel, TQ=TQ, NT=NT, NV=NV), in_...  43.3 us
    unnamed x33, local copies, waits for them, and re-layouts  14.1 us
    slice x2, local copies, waits for them, and re-layouts, per_device(): near_keys = near_kv[:, 0].reshape(3 * patch_rows, local_heads, VIT_HD)  7.14 us
    concatenate x1, other arithmetic, extended(): jnp.concatenate([lax.ppermute(tail, axis, [(i, (i + 1) % count) for i in...  6.68 us
    ppermute x1, starting transfers between devices, extended(): lax.ppermute(head, axis, [((i + 1) % count, i) for i in range(ends)])  5.12 us
    sub x1, matrix products, per_device(): weights = jax.nn.softmax(scores, axis=-1).astype(jnp.bfloat16)  4.89 us
    dot_general x1, matrix products, per_device(): jnp.dot(normed, qkv_weight.reshape(model_width, 3 * head_cols), preferred...  4.22 us
  transfers between devices with their start and end apart: 3, of which 2 were waited for; matrix products, arithmetic and copies ran while one was open for 8% of the time, Pallas kernels for 0%

profile of v1, /device:TPU:1, one launch (start us, length us, event | category | flops | bytes accessed | tf_op | source)
XLA Modules:
  0.0 176.8 jit_solution(8490855074141690996)
XLA Ops:
  0.6 1.3 convert_reduce_fusion.1
  2.0 1.3 fusion.11
  3.3 8.2 %copy.38 = bf16[1280,3,640]{0,2,1:T(8,128)(2,1)} copy(bf16[1280,3,640]{2,0,1:T(8,128)(2,1)} %param.17) | data formatting | bytes 9830400 | tf_op args[3]
  11.6 4.2 %convolution_convert_fusion = bf16[192,1920]{1,0:T(8,128)(2,1)S(1)} fusion(bf16[1280,1920]{0,1:T(8,128)(2,1)} %bitcast.39, bf16[192,1280]{1,0:T(8,128)(2,1)S(1)} %copy-done.1, f32[1280]{0:T(1024)S(1)} %copy-done.13, f32[1280]{0:T(1024)S(1)} %copy-done.14, f32[192]{0:T(256)S(1)} %add_rsqrt_fusion.1, f32[192]{0:T(256)S(1)} %broadcast_multiply_fusion.1), kind=kOutput, calls=%fused_computation.5 | convolution fusion | flops 945561600 | bytes 6155776 | tf_op jit(solution)/shard_map/dot_general | solution.py:372
  16.6 5.1 %collective-permute-start.1 = (bf16[192,2,640]{2,1,0:T(2,128)(2,1)S(1)}, bf16[192,2,640]{2,1,0:T(2,128)(2,1)}, u32[]{:S(2)}, u32[]{:S(2)}) collective-permute-start(bf16[192,2,640]{2,1,0:T(2,128)(2,1)S(1)} %slice.44), channel_id=1, source_target_pairs={{2,0},{4,2},{6,4},{8,6},{10,8},{12,10},{14,12},{16,14},{18,16},{20... | collective-permute-start | bytes 1474568 | tf_op jit(solution)/shard_map/ppermute | solution.py:324
  21.7 1.9 %collective-permute-start = (bf16[192,2,640]{2,1,0:T(2,128)(2,1)S(1)}, bf16[192,2,640]{2,1,0:T(2,128)(2,1)}, u32[]{:S(2)}, u32[]{:S(2)}) collective-permute-start(bf16[192,2,640]{2,1,0:T(2,128)(2,1)S(1)} %slice.44), channel_id=1, source_target_pairs={{0,2},{2,4},{4,6},{6,8},{8,10},{10,12},{12,14},{14,16},{16,18},{18... | collective-permute-start | bytes 1474568 | tf_op jit(solution)/shard_map/ppermute | solution.py:322
  25.4 1.1 slice.46
  26.6 2.0 %copy.41 = bf16[192,1,640]{0,2,1:T(8,128)(2,1)} copy(bf16[192,1,640]{2,1,0:T(2,128)(2,1)} %slice.46) | data formatting | bytes 491520 | tf_op jit(solution)/shard_map/slice | solution.py:383
  29.4 6.7 %pad_maximum_fusion = bf16[576,2,640]{2,1,0:T(2,128)(2,1)S(1)} fusion(bf16[192,2,640]{2,1,0:T(2,128)(2,1)} %collective-permute-done.1, bf16[192,2,640]{2,1,0:T(2,128)(2,1)S(1)} %slice.44, bf16[192,2,640]{2,1,0:T(2,128)(2,1)} %collective-permute-done), kind=kLoop, calls=%fused_computation.15 | loop fusion | flops 1474560 | bytes 2949120 | tf_op jit(solution)/shard_map/concatenate | solution.py:320
  36.1 2.9 %fusion.44 = (bf16[576,1,640]{2,1,0:T(2,128)(2,1)}, bf16[576,1,640]{2,1,0:T(2,128)(2,1)S(1)}) fusion(bf16[576,2,640]{2,1,0:T(2,128)(2,1)S(1)} %pad_maximum_fusion), kind=kLoop, calls=%fused_computation.85 | loop fusion | bytes 2949120 | tf_op jit(solution)/shard_map/slice | solution.py:384
  39.0 4.2 %copy.42 = bf16[576,1,640]{0,2,1:T(8,128)(2,1)} copy(bf16[576,1,640]{2,1,0:T(2,128)(2,1)} %get-tuple-element.12) | data formatting | bytes 1474560 | tf_op jit(solution)/shard_map/slice | solution.py:384
  43.2 3.1 %copy.39 = bf16[576,1,640]{0,2,1:T(8,128)(2,1)} copy(bf16[576,1,640]{2,1,0:T(2,128)(2,1)S(1)} %get-tuple-element.13) | data formatting | bytes 1474560 | tf_op jit(solution)/shard_map/slice | solution.py:385
  46.3 4.9 %fusion.47 = (f32[8,192]{1,0:T(8,128)S(1)}, f32[8,192,576]{2,1,0:T(8,128)}) fusion(pred[192,576]{1,0:T(8,128)(4,1)S(1)} %broadcast_compare_fusion, bf16[192,8,80]{0,2,1:T(8,128)(2,1)} %bitcast.44, bf16[576,8,80]{0,2,1:T(8,128)(2,1)} %bitcast.41), kind=kOutput, calls=%fused_computation.88 | convolution fusion | flops 145097280 | bytes 4638720 | tf_op jit(solution)/shard_map/sub | solution.py:391
  51.2 3.1 %fusion.6 = bf16[8,80,192]{2,1,0:T(8,128)(2,1)S(1)} fusion(bf16[576,8,80]{0,2,1:T(8,128)(2,1)S(1)} %bitcast.42, f32[8,192,576]{2,1,0:T(8,128)} %get-tuple-element.20, f32[8,192]{1,0:T(8,128)S(1)} %get-tuple-element.19), kind=kOutput, calls=%fused_computation.21 | convolution fusion | flops 143450112 | bytes 4528128 | tf_op jit(solution)/shard_map/hqk,khd->qhd/dot_general | solution.py:392
  54.9 1.0 broadcast_in_dim.45
  55.9 3.7 %all-to-all-start = ((bf16[2,192,1280]{2,1,0:T(8,128)(2,1)}), bf16[2,192,1280]{2,1,0:T(8,128)(2,1)S(1)}, u32[]{:S(2)}, u32[]{:S(2)}) async-start(bf16[2,192,1280]{2,1,0:T(8,128)(2,1)} %broadcast_in_dim.45), calls=%async_computation | async-start | bytes 1966080 | tf_op jit(solution)/shard_map/all_to_all | solution.py:333
  60.4 0.7 copy.46.qpos_ref
  61.2 5.8 %copy.48 = bf16[640,8,2,256]{3,1,2,0:T(8,128)(2,1)} copy(bf16[640,8,2,256]{3,2,1,0:T(2,128)(2,1)} %bitcast.38) | data formatting | bytes 10485760
  67.6 1.1 convolution_convert_fusion.2.q_ref
  68.7 3.0 %all-to-all-done = bf16[2,192,1280]{2,1,0:T(8,128)(2,1)S(1)} async-done(((bf16[2,192,1280]{2,1,0:T(8,128)(2,1)}), bf16[2,192,1280]{2,1,0:T(8,128)(2,1)S(1)}, u32[]{:S(2)}, u32[]{:S(2)}) %all-to-all-start) | async-done | bytes 983072 | tf_op jit(solution)/shard_map/all_to_all | solution.py:333
  73.2 3.5 %convolution_convert_fusion.4.vis_ref = bf16[48,512]{1,0:T(8,128)(2,1)S(1)} fusion(bf16[48,5120]{1,0:T(8,128)(2,1)S(1)} %reshape.169, bf16[5120,512]{1,0:T(8,128)(2,1)} %bitcast.37), kind=kOutput, calls=%fused_computation.27 | convolution fusion | flops 251682816 | bytes 5783552 | tf_op jit(solution)/shard_map/dot_general | solution.py:399
  77.3 53.9 %gather.1 = (bf16[64,136,512]{2,1,0:T(8,128)(2,1)}, bf16[64,48,512]{2,1,0:T(8,128)(2,1)}) custom-call(bf16[136,512]{1,0:T(8,128)(2,1)} %fusion.29.text_ref, bf16[48,512]{1,0:T(8,128)(2,1)} %copy-done.5), custom_call_target="tpu_custom_call" | custom-call | tf_op jit(solution)/shard_map/gather/pallas_call | solution.py:299
  131.2 0.9 slice_convert_fusion
  133.3 43.3 %attend.1 = bf16[128,2048]{1,0:T(8,128)(2,1)} custom-call(bf16[128,2048]{1,0:T(8,128)(2,1)} %convolution_convert_fusion.2.q_ref, bf16[64,136,512]{2,1,0:T(8,128)(2,1)} %get-tuple-element.4.kvt_ref, bf16[3,64,16,512]{3,2,1,0:T(8,128)(2,1)} %bitcast.40, s32[128,1]{1,0:T(8,128)} %copy.46.qpos_ref, s32[12,1024]{1,0:T(8,128)} %add_add_fusion.kp_ref, ...), custom_call_target="tpu_custom_call" | custom-call | tf_op jit(solution)/shard_map/attend/pallas_call | solution.py:115
  (73 shorter events, 8.5 us)
Async XLA Ops:
  0.6 53.7 %copy-start = (bf16[640,1280]{1,0:T(8,128)(2,1)S(1)}, bf16[640,1280]{1,0:T(8,128)(2,1)}, u32[]{:S(2)}) copy-start(bf16[640,1280]{1,0:T(8,128)(2,1)} %param.18) | copy-start | bytes 4915204
  3.3 8.3 %copy-start.1 = (bf16[192,1280]{1,0:T(8,128)(2,1)S(1)}, bf16[192,1280]{1,0:T(8,128)(2,1)}, u32[]{:S(2)}) copy-start(bf16[192,1280]{1,0:T(8,128)(2,1)} %param.14) | copy-start | bytes 1474564
  3.3 8.3 %copy-start.13 = (f32[1280]{0:T(1024)S(1)}, f32[1280]{0:T(1024)}, u32[]{:S(2)}) copy-start(f32[1280]{0:T(1024)} %param.16) | copy-start | bytes 15364
  3.3 8.3 %copy-start.14 = (f32[1280]{0:T(1024)S(1)}, f32[1280]{0:T(1024)}, u32[]{:S(2)}) copy-start(f32[1280]{0:T(1024)} %param.15) | copy-start | bytes 15364
  11.6 12.1 %copy-start.10 = (s32[128]{0:T(128)S(1)}, s32[128]{0:T(128)}, u32[]{:S(2)}) copy-start(s32[128]{0:T(128)} %param.23) | copy-start | bytes 1540
  11.6 12.1 %copy-start.11 = (s32[128]{0:T(128)S(1)}, s32[128]{0:T(128)}, u32[]{:S(2)}) copy-start(s32[128]{0:T(128)} %param.25) | copy-start | bytes 1540
  11.6 12.1 %copy-start.12 = (s32[128]{0:T(128)S(1)}, s32[128]{0:T(128)}, u32[]{:S(2)}) copy-start(s32[128]{0:T(128)} %param.24) | copy-start | bytes 1540
  15.8 10.8 %copy-start.6 = (bf16[128,2,256]{2,1,0:T(2,128)(2,1)S(1)}, bf16[128,2,256]{2,1,0:T(2,128)(2,1)}, u32[]{:S(2)}) copy-start(bf16[128,2,256]{2,1,0:T(2,128)(2,1)} %param.27) | copy-start | bytes 393220
  16.6 12.3 %collective-permute-start.1 = (bf16[192,2,640]{2,1,0:T(2,128)(2,1)S(1)}, bf16[192,2,640]{2,1,0:T(2,128)(2,1)}, u32[]{:S(2)}, u32[]{:S(2)}) collective-permute-start(bf16[192,2,640]{2,1,0:T(2,128)(2,1)S(1)} %slice.44), channel_id=1, source_target_pairs={{2,0},{4,2},{6,4},{8,6},{10,8},{12,10},{14,12},{16,14},{18,16},{20... | collective-permute-start | bytes 1474568 | tf_op jit(solution)/shard_map/ppermute | solution.py:324
  21.7 7.7 %collective-permute-start = (bf16[192,2,640]{2,1,0:T(2,128)(2,1)S(1)}, bf16[192,2,640]{2,1,0:T(2,128)(2,1)}, u32[]{:S(2)}, u32[]{:S(2)}) collective-permute-start(bf16[192,2,640]{2,1,0:T(2,128)(2,1)S(1)} %slice.44), channel_id=1, source_target_pairs={{0,2},{2,4},{4,6},{6,8},{8,10},{10,12},{12,14},{14,16},{16,18},{18... | collective-permute-start | bytes 1474568 | tf_op jit(solution)/shard_map/ppermute | solution.py:322
  46.3 4.9 %copy-start.3 = (bf16[576,1,640]{0,2,1:T(8,128)(2,1)S(1)}, bf16[576,1,640]{0,2,1:T(8,128)(2,1)}, u32[]{:S(2)}) copy-start(bf16[576,1,640]{0,2,1:T(8,128)(2,1)} %copy.39) | copy-start | bytes 2211844
  55.9 15.8 %all-to-all-start = ((bf16[2,192,1280]{2,1,0:T(8,128)(2,1)}), bf16[2,192,1280]{2,1,0:T(8,128)(2,1)S(1)}, u32[]{:S(2)}, u32[]{:S(2)}) async-start(bf16[2,192,1280]{2,1,0:T(8,128)(2,1)} %broadcast_in_dim.45), calls=%async_computation | async-start | bytes 1966080 | tf_op jit(solution)/shard_map/all_to_all | solution.py:333
  61.2 6.5 %copy-start.4 = (bf16[128,2048]{1,0:T(8,128)(2,1)S(1)}, bf16[128,2048]{1,0:T(8,128)(2,1)}, u32[]{:S(2)}) copy-start(bf16[128,2048]{1,0:T(8,128)(2,1)} %param.26) | copy-start | bytes 1572868
  61.2 10.7 %copy-start.2 = (bf16[192,1280]{1,0:T(8,128)(2,1)S(1)}, bf16[192,1280]{1,0:T(8,128)(2,1)}, u32[]{:S(2)}) copy-start(bf16[192,1280]{1,0:T(8,128)(2,1)} %param.14) | copy-start | bytes 1474564
  61.2 10.7 %copy-start.7 = (f32[1280]{0:T(1024)S(1)}, f32[1280]{0:T(1024)}, u32[]{:S(2)}) copy-start(f32[1280]{0:T(1024)} %param.19) | copy-start | bytes 15364
  66.9 5.5 %copy-start.8 = (f32[1280]{0:T(1024)S(1)}, f32[1280]{0:T(1024)}, u32[]{:S(2)}) copy-start(f32[1280]{0:T(1024)} %param.21) | copy-start | bytes 15364
  66.9 5.5 %copy-start.9 = (f32[1280]{0:T(1024)S(1)}, f32[1280]{0:T(1024)}, u32[]{:S(2)}) copy-start(f32[1280]{0:T(1024)} %param.20) | copy-start | bytes 15364
  76.6 0.7 copy-start.5

commit v2 on v1

v2 whole, which is shorter than its diff:
```python
import functools
import heapq
import math

import jax
import jax.numpy as jnp
from jax import lax
from jax.experimental import pallas as pl
from jax.experimental.pallas import tpu as pltpu
from jax.sharding import Mesh
from jax.sharding import PartitionSpec as P

MESH = pl.DeviceIdType.MESH


VIT_HD = 80
HEAD_DIM = 128
GROUP = 8
SEQ = ("seq_0", "seq_1", "seq_2")
GRP_SEQ = ("grp", "seq_0", "seq_1", "seq_2")


epsilon = 1e-06
NEG = -1e30
C=math.log2(math.e)/math.sqrt(128)
G=8; D=128
BIG=2**30

def attend_kernel(q_ref, kvt_ref, kvv_ref, qpos_ref, kp_ref, perm_ref, out_ref,
                  kbuf, vbuf, s_sc, x_sc, p_sc, a_sc, o_sc, m_sc, l_sc, srt_sc, sem, *, TQ, NT, NV):
    R=G*TQ
    nq=128//TQ
    KB=1024
    S=kvt_ref.shape[0]
    RB=KB//S
    def copies(h,b):
        out=[]
        for j,buf in ((0,kbuf),(1,vbuf)):
            c=j*256+h*D
            if b<NT:
                src=kvt_ref.at[:,b*RB:(b+1)*RB,c:c+D]
                dst=buf.at[h,b]
            else:
                src=kvv_ref.at[b-NT,:,:,c:c+D]
                dst=buf.at[h,b]
            out.append(pltpu.make_async_copy(src,dst,sem.at[h,b]))
        return out
    for h in range(2):
        for b in range(NT+NV):
            for c in copies(h,b): c.start()
    kmin=jnp.min(kp_ref[...],axis=1,keepdims=True)
    tmin=kmin[0:NT]; vmin=kmin[NT:NT+NV]
    for h in range(2):
        for b in range(NT+NV):
            for c in copies(h,b): c.wait()
        for i in range(nq):
            qp=qpos_ref[i*TQ:(i+1)*TQ,0:1]
            qhi=jnp.max(qp,axis=0,keepdims=True)
            nt=jnp.sum((tmin<=qhi).astype(jnp.int32))
            nv=jnp.sum((vmin<=qhi).astype(jnp.int32))
            n=nt+nv
            q=jnp.concatenate([q_ref[i*TQ:(i+1)*TQ,(h*G+g)*D:(h*G+g+1)*D] for g in range(G)],axis=0)
            def blk(j):
                return jnp.minimum(jnp.where(j<nt,j,j-nt+NT),NT+NV-1)
            def pblk(j):
                return jnp.where(j<n,blk(j),NT+NV)
            def qk(j,t):
                k=kbuf[h,blk(j)].reshape(KB,D)
                s=lax.dot_general(q,k,(((1,),(1,)),((),())),preferred_element_type=jnp.float32)
                bias=jnp.where(kp_ref[pl.ds(pblk(j),1),:]<=qp,0.0,NEG)
                s=s+jnp.concatenate([bias]*G,axis=0)
                s_sc[t]=s
                x=s[:,0:128]
                for c in range(1,KB//128): x=jnp.maximum(x,s[:,c*128:(c+1)*128])
                x_sc[t]=x
            def soft(t):
                m_old=m_sc[:,0:1]
                m_new=jnp.maximum(m_old,jnp.max(x_sc[t],axis=1,keepdims=True))
                mc=m_new*C
                p=jnp.exp2(s_sc[t]*C-mc)
                a=jnp.exp2(m_old*C-mc)
                l=p[:,0:128]
                for c in range(1,KB//128): l=l+p[:,c*128:(c+1)*128]
                l_sc[...]=l_sc[...]*a+l
                p_sc[t]=p.astype(jnp.bfloat16)
                a_sc[t]=jnp.broadcast_to(a,(R,128))
                m_sc[...]=jnp.broadcast_to(m_new,m_sc.shape)
            def pv(j,t):
                v=vbuf[h,blk(jnp.maximum(j,0))].reshape(KB,D)
                o_sc[...]=o_sc[...]*a_sc[t]+jnp.dot(p_sc[t],v,preferred_element_type=jnp.float32)
            m_sc[...]=jnp.full_like(m_sc,NEG)
            l_sc[...]=jnp.zeros_like(l_sc)
            o_sc[...]=jnp.zeros_like(o_sc)
            p_sc[1]=jnp.zeros_like(p_sc[1])
            a_sc[1]=jnp.zeros_like(a_sc[1])
            qk(0,0)
            @pl.loop(0,(n+1)//2)
            def _(jj):
                j=jj*2
                pv(j-1,1); qk(j+1,1); soft(0)
                pv(j,0); qk(j+2,0); soft(1)
            pv(((n+1)//2)*2-1,1)
            o=(o_sc[...]/jnp.sum(l_sc[...],axis=1,keepdims=True)).astype(jnp.bfloat16)
            for g in range(G):
                srt_sc[i*TQ:(i+1)*TQ,g*D:(g+1)*D]=o[g*TQ:(g+1)*TQ]
        out_ref[:,h*1024:(h+1)*1024]=jnp.dot(perm_ref[...],srt_sc[...],preferred_element_type=jnp.float32).astype(jnp.bfloat16)

def attend(q,kvt,kvv,qpos,kp,perm):
    S=kvt.shape[0]; V=kvv.shape[0]*kvv.shape[1]
    KB=1024; RB=KB//S; NT=S*128//KB; NV=V//KB
    kvv4=kvv.reshape(NV,S,RB,512)
    TQ=32
    R=G*TQ
    vm=lambda: pl.BlockSpec(memory_space=pltpu.VMEM)
    hb=lambda: pl.BlockSpec(memory_space=pl.ANY)
    return pl.pallas_call(
        functools.partial(attend_kernel,TQ=TQ,NT=NT,NV=NV),
        in_specs=[vm(),hb(),hb(),vm(),vm(),vm()],
        out_specs=vm(),
        out_shape=jax.ShapeDtypeStruct((128,2048),jnp.bfloat16),
        scratch_shapes=[pltpu.VMEM((2,NT+NV,S,RB,D),jnp.bfloat16),pltpu.VMEM((2,NT+NV,S,RB,D),jnp.bfloat16),
          pltpu.VMEM((2,R,KB),jnp.float32),pltpu.VMEM((2,R,128),jnp.float32),pltpu.VMEM((2,R,KB),jnp.bfloat16),pltpu.VMEM((2,R,128),jnp.float32),
          pltpu.VMEM((R,128),jnp.float32),pltpu.VMEM((R,128),jnp.float32),pltpu.VMEM((R,128),jnp.float32),pltpu.VMEM((128,1024),jnp.bfloat16),
          pltpu.SemaphoreType.DMA((2,NT+NV))],
        compiler_params=pltpu.CompilerParams(vmem_limit_bytes=60<<20),
        name="attend",
    )(q,kvt,kvv4,qpos,kp,perm)


def ring_plan(na, nb):
    free = {}
    heap = []
    count = [0]
    def send(axis, way, a, b, part, at):
        start = max(at, free.get((axis, way), 0.0))
        end = start + (1.0 if part == 0 else 0.5)
        free[(axis, way)] = end
        count[0] += 1
        heapq.heappush(heap, (end + 0.9, count[0], axis, way, a, b, part))
    def spread(axis, size, way, off, at, a, b):
        nxt = off + 1
        if nxt < size // 2:
            part = 0
        elif nxt == size // 2:
            part = 1 if way == 1 else 2
        else:
            return None
        return part
    def go(axis, size, way, off, at, a, b):
        part = spread(axis, size, way, off, at, a, b)
        if part is not None:
            na_, nb_ = (a + way, b) if axis == "a" else (a, b + way)
            send(axis, way, na_, nb_, part, at)
    for way in (1, -1):
        go("a", na, way, 0, 0.0, 0, 0)
    for way in (1, -1):
        go("b", nb, way, 0, 0.0, 0, 0)
    order = []
    halves = {}
    while heap:
        at, _, axis, way, a, b, part = heapq.heappop(heap)
        order.append((axis, way, a, b, part))
        if axis == "a":
            if part == 0:
                go("a", na, way, abs(a), at, a, b)
                for w in (1, -1):
                    go("b", nb, w, 0, at, a, b)
            else:
                key = abs(a)
                halves[("a", key, b)] = halves.get(("a", key, b), 0) + 1
                if halves[("a", key, b)] == 2:
                    for w in (1, -1):
                        go("b", nb, w, 0, at, na // 2, b)
        else:
            if part == 0:
                go("b", nb, way, abs(b), at, a, b)
    return order

def barrier(devices):
    sem = pltpu.get_barrier_semaphore()
    for device in devices:
        pl.semaphore_signal(sem, inc=1, device_id=device, device_id_type=MESH)
    pl.semaphore_wait(sem, len(devices))


def near(y, z, core, ny, nz):
    return [
        {"seq_0": lax.rem(y + 1, ny)},
        {"seq_0": lax.rem(y + ny - 1, ny)},
        {"seq_1": lax.rem(z + 1, nz)},
        {"seq_1": lax.rem(z + nz - 1, nz)},
        {"seq_2": 1 - core},
    ]


class Gather:
    def __init__(self, own, out, cut, send_sem, recv_sem, place, core):
        self.own, self.out, self.rows, self.cut = own, out, own.shape[0], cut
        self.send_sem, self.recv_sem = send_sem, recv_sem
        self.y, self.z, self.ny, self.nz = place
        self.core = core
        self.sizes = (self.nz, self.ny) if core == 0 else (self.ny, self.nz)
        self.plan = ring_plan(*self.sizes)
        self.sent = []
        self.halves = {}
        self.next = 0

    def shard(self, core, dz, dy):
        y = lax.rem(self.y - dy + self.ny, self.ny)
        z = lax.rem(self.z - dz + self.nz, self.nz)
        return (y * self.nz + z) * 2 + core

    def source(self, a, b):
        return self.shard(0, a, b) if self.core == 0 else self.shard(1, b, a)

    def piece(self, ref, part):
        if part == 0:
            return ref
        return ref.at[0 : self.cut] if part == 1 else ref.at[self.cut : self.rows]

    def copy(self, src, index, part, number, device):
        return pltpu.make_async_remote_copy(
            src_ref=self.piece(src, part),
            dst_ref=self.piece(self.out.at[index], part),
            send_sem=self.send_sem.at[number],
            recv_sem=self.recv_sem.at[index, 1 if part == 2 else 0],
            device_id=device,
            device_id_type=MESH,
        )

    def neighbour(self, axis, way):
        if (axis == "a") == (self.core == 0):
            return {"seq_1": lax.rem(self.z + way + self.nz, self.nz)}
        return {"seq_0": lax.rem(self.y + way + self.ny, self.ny)}

    def send(self, src, index, part, device):
        self.copy(src, index, part, len(self.sent), device).start()
        self.sent.append(part)

    def partner(self):
        return {"seq_2": 1 - self.core}

    def begin(self):
        index = self.source(0, 0)
        for axis in ("a", "b"):
            for way in (1, -1):
                self.send(self.own, index, 0, self.neighbour(axis, way))
        self.send(self.own, index, 0, self.partner())

    def wait(self, index, part):
        self.copy(self.own, index, part, 0, self.partner()).wait_recv()

    def step(self, axis, way, a, b, part):
        index = self.source(a, b)
        self.wait(index, part)
        src = self.out.at[index]
        size = self.sizes[0] if axis == "a" else self.sizes[1]
        off = abs(a) if axis == "a" else abs(b)
        done = True
        if part == 0:
            half = 0 if off + 1 < size // 2 else (1 if way == 1 else 2)
            self.send(src, index, half, self.neighbour(axis, way))
        else:
            key = (axis, off, off if axis == "a" else a)
            self.halves[key] = self.halves.get(key, 0) + 1
            done = self.halves[key] == 2
        if done:
            if axis == "a":
                for onward in (1, -1):
                    self.send(src, index, 0, self.neighbour("b", onward))
            self.send(src, index, 0, self.partner())

    def advance(self, count):
        for event in self.plan[self.next : self.next + count]:
            self.step(*event)
        self.next = min(len(self.plan), self.next + count)

    def finish(self):
        self.advance(len(self.plan))
        for dz in range(self.nz):
            for dy in range(self.ny):
                self.wait(self.shard(1 - self.core, dz, dy), 0)
        for number, part in enumerate(self.sent):
            self.copy(self.own, 0, part, number, self.partner()).wait_send()


def norm_rows(x, gain, bias):
    centre = jnp.mean(x, axis=-1, keepdims=True)
    centred = x - centre
    spread = jnp.mean(centred * centred, axis=-1, keepdims=True)
    return centred * lax.rsqrt(spread + epsilon) * gain + bias


def encode_kernel(
    text_ref, patches_ref, norms_ref, own_ids_ref, near_ids_ref, qkv_hbm, proj_hbm, wv_hbm,
    text_out, vis_out, vis_own,
    qkv_w, proj_w, wv, normed, q_sc, keys, values, mixed, part_own, part_far, merged,
    weight_sem, halo_sem, far_sem, ts, tr, vs, vr, loc_sem, *, ny, nz,
):
    f32, bf16 = jnp.float32, jnp.bfloat16
    y, z, core = lax.axis_index("seq_0"), lax.axis_index("seq_1"), lax.axis_index("seq_2")
    far = {"head": 1 - lax.axis_index("head")}
    me = (y * nz + z) * 2 + core
    count = 2 * ny * nz
    rows, width = patches_ref.shape
    cols = q_sc.shape[1]

    def seat(index):
        return {"seq_0": index // (2 * nz), "seq_1": lax.rem(index // 2, nz), "seq_2": lax.rem(index, 2)}

    after, before = seat(lax.rem(me + 1, count)), seat(lax.rem(me + count - 1, count))
    loads = [pltpu.make_async_copy(qkv_hbm.at[j], qkv_w.at[j], weight_sem.at[j]) for j in (1, 2, 0)]
    loads.append(pltpu.make_async_copy(proj_hbm, proj_w, weight_sem.at[3]))
    loads.append(pltpu.make_async_copy(wv_hbm, wv, weight_sem.at[4]))
    for load in loads:
        load.start()
    text_loc = pltpu.make_async_copy(text_ref, text_out.at[me], loc_sem.at[0])
    text_loc.start()
    place = (y, z, ny, nz)
    texts = [Gather(text_ref, text_out, 64, ts, tr, place, c) for c in (0, 1)]
    sights = [Gather(vis_own, vis_out, vis_own.shape[0] // 2, vs, vr, place, c) for c in (0, 1)]

    def on_core(act):
        for c in (0, 1):
            pl.when(core == c)(functools.partial(act, c))

    def pump(count):
        on_core(lambda c: texts[c].advance(count))

    barrier(near(y, z, core, ny, nz) + [after, before, far])
    chunk = rows // 4
    for r in range(0, rows, chunk):
        x = patches_ref[r : r + chunk].astype(f32)
        normed[r : r + chunk] = norm_rows(x, norms_ref[0:1], norms_ref[1:2]).astype(bf16)
    halos = []
    for j, near_ref in ((1, keys), (2, values)):
        loads[j - 1].wait()
        near_ref[1] = jnp.dot(normed[...], qkv_w[j], preferred_element_type=f32).astype(bf16)
        for slot, device in ((0, after), (2, before)):
            number = 2 * (j - 1) + slot // 2
            halos.append(
                pltpu.make_async_remote_copy(
                    src_ref=near_ref.at[1], dst_ref=near_ref.at[slot],
                    send_sem=halo_sem.at[0, number], recv_sem=halo_sem.at[1, number],
                    device_id=device, device_id_type=MESH,
                )
            )
            halos[-1].start()
    on_core(lambda c: texts[c].begin())
    loads[2].wait()
    q_sc[...] = jnp.dot(normed[...], qkv_w[0], preferred_element_type=f32).astype(bf16)
    bias = jnp.where(own_ids_ref[...] == near_ids_ref[...], 0.0, NEG)
    pump(2)
    for halo in halos:
        halo.wait()
    scale = math.log2(math.e) / math.sqrt(VIT_HD)
    for h in range(cols // VIT_HD):
        lo, hi = h * VIT_HD, (h + 1) * VIT_HD
        t0, t1 = lo // 128 * 128, -(-hi // 128) * 128
        lane = lax.broadcasted_iota(jnp.int32, (rows, t1 - t0), 1) + t0
        mine = (lane >= lo) & (lane < hi)
        q = jnp.where(mine, q_sc[:, t0:t1].astype(f32), 0.0).astype(bf16)
        k = keys[:, :, t0:t1].reshape(3 * rows, t1 - t0)
        s = lax.dot_general(q, k, (((1,), (1,)), ((), ())), preferred_element_type=f32) * scale + bias
        e = jnp.exp2(s - jnp.max(s, axis=1, keepdims=True))
        p = (e / jnp.sum(e, axis=1, keepdims=True)).astype(bf16)
        v = values[:, :, t0:t1].reshape(3 * rows, t1 - t0)
        o = jnp.dot(p, v, preferred_element_type=f32)
        if lo == t0:
            mixed[:, t0:t1] = o
        else:
            old = mixed[:, t0:t1] if t1 - t0 == 128 else jnp.concatenate([mixed[:, t0 : t0 + 128], o[:, 128:]], axis=1)
            mixed[:, t0:t1] = jnp.where(mine, o, old)
        pump(2)
    loads[3].wait()
    halves = []
    half = rows // 2
    for i in (0, 1):
        part = slice(i * half, (i + 1) * half)
        part_own[part] = jnp.dot(mixed[part].astype(bf16), proj_w[...], preferred_element_type=f32).astype(bf16)
        halves.append(
            pltpu.make_async_remote_copy(
                src_ref=part_own.at[part], dst_ref=part_far.at[part],
                send_sem=far_sem.at[0, i], recv_sem=far_sem.at[1, i], device_id=far, device_id_type=MESH,
            )
        )
        halves[-1].start()
        pump(2)
    for i in (0, 1):
        pump(4)
        halves[i].wait()
        for r in range(i * half, (i + 1) * half, chunk):
            summed = part_own[r : r + chunk].astype(f32) + part_far[r : r + chunk].astype(f32)
            x = (patches_ref[r : r + chunk].astype(f32) + summed + norms_ref[2:3]).astype(bf16)
            x = norm_rows(x.astype(f32), norms_ref[3:4], norms_ref[4:5])
            for t in range(width // 128):
                merged[t, r : r + chunk] = x[:, t * 128 : (t + 1) * 128]
    loads[4].wait()
    tokens = rows // 4
    total = jnp.zeros((tokens, wv.shape[1]), f32)
    for j in range(4):
        row = [merged[t, pl.ds(j, tokens, stride=4), :] for t in range(width // 128)]
        row = jnp.concatenate(row, axis=1).astype(bf16)
        total = total + jnp.dot(row, wv[j * width : (j + 1) * width], preferred_element_type=f32)
    vis_own[...] = total.astype(bf16)
    vis_loc = pltpu.make_async_copy(vis_own, vis_out.at[me], loc_sem.at[1])
    vis_loc.start()

    def close(c):
        sights[c].begin()
        for _ in sights[c].plan:
            sights[c].advance(1)
            texts[c].advance(1)
        texts[c].finish()
        sights[c].finish()

    on_core(close)
    text_loc.wait()
    vis_loc.wait()


def encode(text, patches, norms, own_ids, near_ids, qkv, proj, wv, ny, nz):
    n = ny * nz * 2
    rows, width = patches.shape
    cols = qkv.shape[2]
    tokens = rows // 4
    bf16, f32 = jnp.bfloat16, jnp.float32
    hbm = pl.BlockSpec(memory_space=pl.ANY)
    vmem = pl.BlockSpec(memory_space=pltpu.VMEM)
    dma = pltpu.SemaphoreType.DMA
    return pl.pallas_call(
        functools.partial(encode_kernel, ny=ny, nz=nz),
        in_specs=[vmem] * 5 + [hbm] * 3,
        out_specs=[hbm, hbm, vmem],
        out_shape=[
            jax.ShapeDtypeStruct((n, *text.shape), bf16),
            jax.ShapeDtypeStruct((n, tokens, wv.shape[1]), bf16),
            jax.ShapeDtypeStruct((tokens, wv.shape[1]), bf16),
        ],
        scratch_shapes=[
            pltpu.VMEM(qkv.shape, bf16), pltpu.VMEM(proj.shape, bf16), pltpu.VMEM(wv.shape, bf16),
            pltpu.VMEM((rows, width), bf16), pltpu.VMEM((rows, cols), bf16),
            pltpu.VMEM((3, rows, cols), bf16), pltpu.VMEM((3, rows, cols), bf16),
            pltpu.VMEM((rows, cols), f32), pltpu.VMEM((rows, width), bf16), pltpu.VMEM((rows, width), bf16),
            pltpu.VMEM((width // 128, rows, 128), f32),
            dma((5,)), dma((2, 4)), dma((2, 2)),
            dma((2 * n + 16,)), dma((n, 2)), dma((2 * n + 16,)), dma((n, 2)), dma((2,)),
        ],
        compiler_params=pltpu.CompilerParams(collective_id=1, has_side_effects=True, vmem_limit_bytes=60 << 20),
        name="encode",
    )(text, patches, norms, own_ids, near_ids, qkv, proj, wv)


def per_device(
    patches, ln_gain, ln_bias, qkv_weight, proj_weight, proj_bias, merge_gain, merge_bias, visual_kv_weight,
    image_tokens, text_before, text_order, queries, text_kv,
):
    seq_index = lax.axis_index(SEQ)
    ny, nz = lax.axis_size("seq_0"), lax.axis_size("seq_1")
    patch_rows = patches.shape[0]
    merged_rows = patch_rows // 4
    total_patches = patch_rows * lax.axis_size(SEQ)
    token_ends = jnp.cumsum(image_tokens)
    near_index = seq_index * patch_rows - patch_rows + jnp.arange(3 * patch_rows, dtype=jnp.int32)
    near_ids = jnp.sum((near_index[:, None] >= 4 * token_ends[None, :]).astype(jnp.int32), axis=1)
    near_ids = jnp.where((near_index >= 0) & (near_index < total_patches), near_ids, -1)
    own_ids = near_ids[patch_rows : 2 * patch_rows]
    text_pos = text_order + jnp.sum(
        jnp.where(text_before[None, :] <= text_order[:, None], image_tokens[None, :], 0), axis=1
    )
    image_starts = token_ends - image_tokens
    steps_before = text_before - jnp.concatenate([jnp.zeros((1,), jnp.int32), text_before[:-1]])
    tokens = queries.shape[0]
    rank = jnp.sum((text_order[None, :] < text_order[:, None]).astype(jnp.int32), axis=1)
    hot = (rank[None, :] == jnp.arange(tokens, dtype=jnp.int32)[:, None]).astype(jnp.bfloat16)
    q = jnp.dot(hot, queries, preferred_element_type=jnp.float32).astype(jnp.bfloat16)
    places = jnp.stack([text_pos // 128, text_pos % 128]).astype(jnp.bfloat16)
    places = lax.dot_general(places, hot, (((1,), (1,)), ((), ())), preferred_element_type=jnp.float32)
    kv = jnp.dot(hot, text_kv.reshape(tokens, -1), preferred_element_type=jnp.float32).astype(jnp.bfloat16)
    places_rows = jnp.pad(places.astype(jnp.bfloat16), ((0, 6), (0, kv.shape[1] - tokens)))
    norms = jnp.stack([ln_gain, ln_bias, proj_bias, merge_gain, merge_bias])
    all_text, all_vis, visual_kv = encode(
        jnp.concatenate([kv, places_rows], axis=0), patches, norms, own_ids[:, None], near_ids[None, :],
        jnp.transpose(qkv_weight, (1, 0, 2)), proj_weight,
        visual_kv_weight.reshape(visual_kv_weight.shape[0], -1), ny, nz,
    )
    visual_kv = visual_kv.reshape(merged_rows, 2, -1)
    key_pos = all_text[:, tokens : tokens + 2, :tokens].astype(jnp.int32)
    key_pos = key_pos[:, 0] * 128 + key_pos[:, 1]
    sources = key_pos.shape[0]
    blocks = sources * tokens // 1024
    key_pos = key_pos.reshape(sources, blocks, tokens // blocks).transpose(1, 0, 2).reshape(blocks, 1024)
    visual_index = jnp.arange(sources * merged_rows, dtype=jnp.int32)
    all_vis_pos = visual_index + jnp.sum(
        jnp.where(image_starts[None, :] <= visual_index[:, None], steps_before[None, :], 0), axis=1
    )
    kp = jnp.concatenate([key_pos, all_vis_pos.reshape(-1, 1024), jnp.full((1, 1024), BIG, jnp.int32)], axis=0)
    places = places.astype(jnp.int32)
    q_pos = (places[0] * 128 + places[1])[:, None]
    attended = attend(q, all_text, all_vis, q_pos, kp, hot.T)
    return (attended, visual_kv)


def solution(mesh):
    split = Mesh(
        mesh.devices.reshape(mesh.shape["grp"], 4, 8, 2, mesh.shape["head"]),
        ("grp", "seq_0", "seq_1", "seq_2", "head"),
    )
    in_specs = (
        P(GRP_SEQ, None),
        P(),
        P(),
        P(None, None, "head"),
        P("head", None),
        P(),
        P(),
        P(),
        P(None, None, "head"),
        P("grp"),
        P("grp"),
        P(GRP_SEQ),
        P(GRP_SEQ, "head"),
        P(GRP_SEQ, None, "head"),
    )
    out_specs = (P(GRP_SEQ, "head"), P(GRP_SEQ, None, "head"))
    return jax.shard_map(
        per_device, mesh=split, in_specs=in_specs, out_specs=out_specs, check_vma=False
    )
```

time: 179 us -> 143 us (0.80)
  Pallas kernels: 97.2 us -> 120 us
  local copies, waits for them, and re-layouts: 31.6 us -> 11 us
  matrix products: 17.6 us -> 1.47 us
  starting transfers between devices: 10.8 us -> 0 us
  other arithmetic: 14.8 us -> 7.06 us
  waiting for transfers between devices: 3.53 us -> 0 us
    pallas_call x1, Pallas kernels: 53.9 us -> 76.8 us  [encode(): pl.pallas_call(functools.partial(encode_kernel, ny=ny, nz=nz), in_specs=[...]
    slice x6 -> x0, local copies, waits for them, and re-layouts: 13.9 us -> none  [the longest x2 7.14 us: per_device(): near_keys = near_kv[:, 0].reshape(3 * patch_rows, local_heads, VIT_HD)]
    dot_general x4 -> x0, matrix products: 11.3 us -> none  [the longest x1 4.22 us: per_device(): jnp.dot(normed, qkv_weight.reshape(model_width, 3 * head_cols), preferred...]
    unnamed x33 -> x16, local copies, waits for them, and re-layouts: 14.1 us -> 6.78 us
    ppermute x2 -> x0, starting transfers between devices: 7.04 us -> none  [the longest x1 5.12 us: extended(): lax.ppermute(head, axis, [((i + 1) % count, i) for i in range(ends)])]
    concatenate x1 -> x0, other arithmetic: 6.68 us -> none  [extended(): jnp.concatenate([lax.ppermute(tail, axis, [(i, (i + 1) % count) for i in...]
    sub x1 -> x0, matrix products: 4.89 us -> none  [per_device(): weights = jax.nn.softmax(scores, axis=-1).astype(jnp.bfloat16)]
    all_to_all x1 -> x0, starting transfers between devices: 3.75 us -> none  [sent_to_all(): lax.all_to_all(jnp.broadcast_to(shard[None], (size, *shard.shape)), axis,...]
  transfers between devices with their start and end apart: 3 -> 0, of which waited for: 2 -> 0; matrix products, arithmetic and copies ran while one was open for 8% -> 0% of each run, Pallas kernels for 0% -> 0%
where the time goes in v2:
time: 143 us; the launch traced here: 140 us
  Pallas kernels  120 us (84%)
  local copies, waits for them, and re-layouts  11 us (8%)
  other arithmetic  7.06 us (5%)
  matrix products  1.47 us (1%)
    pallas_call x1, Pallas kernels, encode(): pl.pallas_call(functools.partial(encode_kernel, ny=ny, nz=nz), in_specs=[...  76.8 us
    pallas_call x1, Pallas kernels, attend(): pl.pallas_call(functools.partial(attend_kernel, TQ=TQ, NT=NT, NV=NV), in_...  43.3 us
    unnamed x16, local copies, waits for them, and re-layouts  6.78 us

profile of v2, /device:TPU:1, one launch (start us, length us, event | category | flops | bytes accessed | tf_op | source)
XLA Modules:
  0.0 140.4 jit_solution(18051795682786379933)
XLA Ops:
  0.7 0.8 copy.29
  1.5 0.2 reduce-window.7
  1.8 0.8 fusion.14
  2.6 0.3 convert_reduce_fusion
  2.9 0.8 copy.30.own_ids_ref
  3.7 0.6 and_select_fusion.near_ids_ref
  4.3 0.9 select_reduce_fusion.1
  5.2 0.7 convert_bitcast_fusion
  5.9 0.1 fusion.13
  6.0 0.9 copy.35
  6.9 0.2 convolution_convert_fusion.1
  7.1 0.7 fusion.1.text_ref
  7.8 5.8 %copy.36 = bf16[640,8,2,256]{3,1,2,0:T(8,128)(2,1)} copy(bf16[640,8,2,256]{3,2,1,0:T(2,128)(2,1)} %bitcast.23) | data formatting | bytes 10485760
  13.7 0.7 stack.38.norms_ref
  14.4 76.8 %encode.1 = (bf16[64,136,512]{2,1,0:T(8,128)(2,1)}, bf16[64,48,512]{2,1,0:T(8,128)(2,1)}, bf16[48,512]{1,0:T(8,128)(2,1)}) custom-call(bf16[136,512]{1,0:T(8,128)(2,1)} %fusion.1.text_ref, bf16[192,1280]{1,0:T(8,128)(2,1)} %patches_ref.1, f32[5,1280]{1,0:T(8,128)} %stack.38.norms_ref, s32[192,1]{1,0:T(8,128)} %copy.30.own_ids_ref, ...), custom_call_target="tpu_custom_call" | custom-call | tf_op jit(solution)/shard_map/encode/pallas_call | solution.py:431
  91.2 0.9 slice_convert_fusion
  92.4 0.2 reshape.114
  92.6 0.5 select_reduce_fusion
  93.2 0.7 add_add_fusion.kp_ref
  93.9 0.7 copy.34.qpos_ref
  94.6 1.2 convolution_convert_fusion.q_ref
  95.8 0.7 fusion.3.perm_ref
  96.5 43.3 %attend.1 = bf16[128,2048]{1,0:T(8,128)(2,1)} custom-call(bf16[128,2048]{1,0:T(8,128)(2,1)} %convolution_convert_fusion.q_ref, bf16[64,136,512]{2,1,0:T(8,128)(2,1)} %get-tuple-element.5.kvt_ref, bf16[3,64,16,512]{3,2,1,0:T(8,128)(2,1)} %bitcast.25, s32[128,1]{1,0:T(8,128)} %copy.34.qpos_ref, s32[12,1024]{1,0:T(8,128)} %add_add_fusion.kp_ref, ...), custom_call_target="tpu_custom_call" | custom-call | tf_op jit(solution)/shard_map/attend/pallas_call | solution.py:116
  139.8 0.6 reshape.115
  (32 shorter events, 0.6 us)
Async XLA Ops:
  0.6 94.0 %copy-start = (bf16[128,2048]{1,0:T(8,128)(2,1)S(1)}, bf16[128,2048]{1,0:T(8,128)(2,1)}, u32[]{:S(2)}) copy-start(bf16[128,2048]{1,0:T(8,128)(2,1)} %param.26) | copy-start | bytes 1572868
  7.8 5.8 %copy-start.2 = (f32[1280]{0:T(1024)S(1)}, f32[1280]{0:T(1024)}, u32[]{:S(2)}) copy-start(f32[1280]{0:T(1024)} %param.15) | copy-start | bytes 15364
  7.8 5.8 %copy-start.3 = (f32[1280]{0:T(1024)S(1)}, f32[1280]{0:T(1024)}, u32[]{:S(2)}) copy-start(f32[1280]{0:T(1024)} %param.16) | copy-start | bytes 15364
  7.8 5.9 %copy-start.4 = (f32[1280]{0:T(1024)S(1)}, f32[1280]{0:T(1024)}, u32[]{:S(2)}) copy-start(f32[1280]{0:T(1024)} %param.19) | copy-start | bytes 15364
  7.8 5.9 %copy-start.5 = (f32[1280]{0:T(1024)S(1)}, f32[1280]{0:T(1024)}, u32[]{:S(2)}) copy-start(f32[1280]{0:T(1024)} %param.20) | copy-start | bytes 15364
  7.8 5.9 %copy-start.6 = (f32[1280]{0:T(1024)S(1)}, f32[1280]{0:T(1024)}, u32[]{:S(2)}) copy-start(f32[1280]{0:T(1024)} %param.21) | copy-start | bytes 15364
  96.5 43.3 %copy-start.1 = (bf16[48,512]{1,0:T(8,128)(2,1)S(1)}, bf16[48,512]{1,0:T(8,128)(2,1)}, u32[]{:S(2)}) copy-start(bf16[48,512]{1,0:T(8,128)(2,1)} %get-tuple-element.7) | copy-start | bytes 147460

commit v3 on v2

--- a/solution.py
+++ b/solution.py
@@ -22,112 +22,160 @@
 
 epsilon = 1e-06
 NEG = -1e30
-C=math.log2(math.e)/math.sqrt(128)
-G=8; D=128
-BIG=2**30
-
-def attend_kernel(q_ref, kvt_ref, kvv_ref, qpos_ref, kp_ref, perm_ref, out_ref,
-                  kbuf, vbuf, s_sc, x_sc, p_sc, a_sc, o_sc, m_sc, l_sc, srt_sc, sem, *, TQ, NT, NV):
-    R=G*TQ
-    nq=128//TQ
-    KB=1024
-    S=kvt_ref.shape[0]
-    RB=KB//S
-    def copies(h,b):
-        out=[]
-        for j,buf in ((0,kbuf),(1,vbuf)):
-            c=j*256+h*D
-            if b<NT:
-                src=kvt_ref.at[:,b*RB:(b+1)*RB,c:c+D]
-                dst=buf.at[h,b]
-            else:
-                src=kvv_ref.at[b-NT,:,:,c:c+D]
-                dst=buf.at[h,b]
-            out.append(pltpu.make_async_copy(src,dst,sem.at[h,b]))
-        return out
+SCALE = math.log2(math.e) / math.sqrt(HEAD_DIM)
+BIG = 2**30
+
+
+def attend_kernel(
+    q_ref, text_ref, vis_ref, qpos_ref, kp_ref, perm_ref, out_ref,
+    kbuf, vbuf, s_sc, x_sc, p_sc, a_sc, o_sc, m_sc, srt_sc, sem, *, tile, texts, sights,
+):
+    f32, bf16 = jnp.float32, jnp.bfloat16
+    d = HEAD_DIM
+    rows = GROUP * tile
+    blocks = texts + sights
+    sources = text_ref.shape[0]
+    ranks = kbuf.shape[3]
+    size = sources * ranks
+    tokens = q_ref.shape[0]
+
+    def copies(h, b):
+        if b < texts:
+            src = text_ref.at[:, b * ranks : (b + 1) * ranks]
+        else:
+            src = vis_ref.at[b - texts]
+        return [
+            pltpu.make_async_copy(src.at[:, :, j * 2 * d + h * d : j * 2 * d + (h + 1) * d], buf.at[h, b, :, :, 0:d], sem.at[h, j, b])
+            for j, buf in ((0, kbuf), (1, vbuf))
+        ]
+
+    order = sorted(range(blocks), key=lambda b: (b + 0.5) / texts if b < texts else (b - texts + 0.4) / sights)
     for h in range(2):
-        for b in range(NT+NV):
-            for c in copies(h,b): c.start()
-    kmin=jnp.min(kp_ref[...],axis=1,keepdims=True)
-    tmin=kmin[0:NT]; vmin=kmin[NT:NT+NV]
+        for b in order:
+            for copy in copies(h, b):
+                copy.start()
+    heads = kp_ref.shape[0]
+    kp = jnp.concatenate([kp_ref[...].astype(f32), jnp.zeros((16 - heads, size), f32)], axis=0)
+    columns = [jnp.transpose(kp[:, t * d : (t + 1) * d]) for t in range(size // d)]
+    qrow = qpos_ref[...].astype(f32)
+    for b in range(blocks + 1):
+        for t in range(size // d):
+            col = jnp.broadcast_to(columns[t][:, b : b + 1], (d, d))
+            mask = jnp.where(col <= qrow, 0.0, NEG).astype(bf16)
+            for h in range(2):
+                kbuf[h, b, t * d // ranks : (t + 1) * d // ranks, :, d:] = mask.reshape(d // ranks, ranks, d)
+    ones = jnp.ones((sources, ranks, d), bf16)
     for h in range(2):
-        for b in range(NT+NV):
-            for c in copies(h,b): c.wait()
-        for i in range(nq):
-            qp=qpos_ref[i*TQ:(i+1)*TQ,0:1]
-            qhi=jnp.max(qp,axis=0,keepdims=True)
-            nt=jnp.sum((tmin<=qhi).astype(jnp.int32))
-            nv=jnp.sum((vmin<=qhi).astype(jnp.int32))
-            n=nt+nv
-            q=jnp.concatenate([q_ref[i*TQ:(i+1)*TQ,(h*G+g)*D:(h*G+g+1)*D] for g in range(G)],axis=0)
-            def blk(j):
-                return jnp.minimum(jnp.where(j<nt,j,j-nt+NT),NT+NV-1)
-            def pblk(j):
-                return jnp.where(j<n,blk(j),NT+NV)
-            def qk(j,t):
-                k=kbuf[h,blk(j)].reshape(KB,D)
-                s=lax.dot_general(q,k,(((1,),(1,)),((),())),preferred_element_type=jnp.float32)
-                bias=jnp.where(kp_ref[pl.ds(pblk(j),1),:]<=qp,0.0,NEG)
-                s=s+jnp.concatenate([bias]*G,axis=0)
-                s_sc[t]=s
-                x=s[:,0:128]
-                for c in range(1,KB//128): x=jnp.maximum(x,s[:,c*128:(c+1)*128])
-                x_sc[t]=x
-            def soft(t):
-                m_old=m_sc[:,0:1]
-                m_new=jnp.maximum(m_old,jnp.max(x_sc[t],axis=1,keepdims=True))
-                mc=m_new*C
-                p=jnp.exp2(s_sc[t]*C-mc)
-                a=jnp.exp2(m_old*C-mc)
-                l=p[:,0:128]
-                for c in range(1,KB//128): l=l+p[:,c*128:(c+1)*128]
-                l_sc[...]=l_sc[...]*a+l
-                p_sc[t]=p.astype(jnp.bfloat16)
-                a_sc[t]=jnp.broadcast_to(a,(R,128))
-                m_sc[...]=jnp.broadcast_to(m_new,m_sc.shape)
-            def pv(j,t):
-                v=vbuf[h,blk(jnp.maximum(j,0))].reshape(KB,D)
-                o_sc[...]=o_sc[...]*a_sc[t]+jnp.dot(p_sc[t],v,preferred_element_type=jnp.float32)
-            m_sc[...]=jnp.full_like(m_sc,NEG)
-            l_sc[...]=jnp.zeros_like(l_sc)
-            o_sc[...]=jnp.zeros_like(o_sc)
-            p_sc[1]=jnp.zeros_like(p_sc[1])
-            a_sc[1]=jnp.zeros_like(a_sc[1])
-            qk(0,0)
-            @pl.loop(0,(n+1)//2)
-            def _(jj):
-                j=jj*2
-                pv(j-1,1); qk(j+1,1); soft(0)
-                pv(j,0); qk(j+2,0); soft(1)
-            pv(((n+1)//2)*2-1,1)
-            o=(o_sc[...]/jnp.sum(l_sc[...],axis=1,keepdims=True)).astype(jnp.bfloat16)
-            for g in range(G):
-                srt_sc[i*TQ:(i+1)*TQ,g*D:(g+1)*D]=o[g*TQ:(g+1)*TQ]
-        out_ref[:,h*1024:(h+1)*1024]=jnp.dot(perm_ref[...],srt_sc[...],preferred_element_type=jnp.float32).astype(jnp.bfloat16)
-
-def attend(q,kvt,kvv,qpos,kp,perm):
-    S=kvt.shape[0]; V=kvv.shape[0]*kvv.shape[1]
-    KB=1024; RB=KB//S; NT=S*128//KB; NV=V//KB
-    kvv4=kvv.reshape(NV,S,RB,512)
-    TQ=32
-    R=G*TQ
-    vm=lambda: pl.BlockSpec(memory_space=pltpu.VMEM)
-    hb=lambda: pl.BlockSpec(memory_space=pl.ANY)
+        kbuf[h, blocks, :, :, 0:d] = jnp.zeros((sources, ranks, d), bf16)
+        for b in range(blocks):
+            vbuf[h, b, :, :, d:] = ones
+    first = jnp.min(kp_ref[...], axis=1, keepdims=True)
+    lane = lax.broadcasted_iota(jnp.int32, (tile, tokens), 1)
+    row = lax.broadcasted_iota(jnp.int32, (tile, tokens), 0)
+    qall = qpos_ref[...]
+    for h in range(2):
+        seen_text, seen_vis = 0, texts
+        for i in range(tokens // tile):
+            qhi = jnp.max(qall[:, i * tile : (i + 1) * tile], axis=1, keepdims=True)
+            visible = (first <= qhi).astype(jnp.int32)
+            nt = jnp.sum(visible[0:texts])
+            nv = jnp.sum(visible[texts:blocks])
+            n = nt + nv
+
+            def arrive(b):
+                for j, buf in ((0, kbuf), (1, vbuf)):
+                    ref = buf.at[h, b, :, :, 0:d]
+                    pltpu.make_async_copy(ref, ref, sem.at[h, j, b]).wait()
+
+            pl.loop(seen_text, nt)(arrive)
+            pl.loop(seen_vis, texts + nv)(arrive)
+            seen_text, seen_vis = nt, texts + nv
+            q = jnp.concatenate(
+                [q_ref[i * tile : (i + 1) * tile, (h * GROUP + g) * d : (h * GROUP + g + 1) * d] for g in range(GROUP)], axis=0
+            )
+            own = (lane == row + i * tile).astype(f32).astype(bf16)
+            q = jnp.concatenate([q, jnp.concatenate([own] * GROUP, axis=0)], axis=1)
+
+            def block(j):
+                return jnp.minimum(jnp.where(j < nt, j, j - nt + texts), blocks - 1)
+
+            def scores(j, slot):
+                k = kbuf[h, jnp.where(j < n, block(j), blocks)].reshape(size, 2 * d)
+                s = lax.dot_general(q, k, (((1,), (1,)), ((), ())), preferred_element_type=f32)
+                s_sc[slot] = s
+                x = s[:, 0:d]
+                for c in range(1, size // d):
+                    x = jnp.maximum(x, s[:, c * d : (c + 1) * d])
+                x_sc[slot] = x
+
+            def weigh(slot):
+                old = m_sc[:, 0:1]
+                new = jnp.maximum(old, jnp.max(x_sc[slot], axis=1, keepdims=True))
+                top = new * SCALE
+                p_sc[slot] = jnp.exp2(s_sc[slot] * SCALE - top).astype(bf16)
+                a_sc[slot] = jnp.broadcast_to(jnp.exp2(old * SCALE - top), (rows, 2 * d))
+                m_sc[...] = jnp.broadcast_to(new, m_sc.shape)
+
+            def add(j, slot):
+                v = vbuf[h, block(jnp.maximum(j, 0))].reshape(size, 2 * d)
+                o_sc[...] = o_sc[...] * a_sc[slot] + jnp.dot(p_sc[slot], v, preferred_element_type=f32)
+
+            m_sc[...] = jnp.full_like(m_sc, NEG)
+            o_sc[...] = jnp.zeros_like(o_sc)
+            p_sc[1] = jnp.zeros_like(p_sc[1])
+            a_sc[1] = jnp.zeros_like(a_sc[1])
+            scores(0, 0)
+
+            @pl.loop(0, (n + 1) // 2)
+            def _(pair):
+                j = pair * 2
+                add(j - 1, 1)
+                scores(j + 1, 1)
+                weigh(0)
+                add(j, 0)
+                scores(j + 2, 0)
+                weigh(1)
+
+            add(((n + 1) // 2) * 2 - 1, 1)
+            o = (o_sc[:, 0:d] / o_sc[:, d : 2 * d]).astype(bf16)
+            for g in range(GROUP):
+                srt_sc[i * tile : (i + 1) * tile, g * d : (g + 1) * d] = o[g * tile : (g + 1) * tile]
+        pl.loop(seen_text, texts)(arrive)
+        pl.loop(seen_vis, blocks)(arrive)
+        width = GROUP * d
+        out_ref[:, h * width : (h + 1) * width] = jnp.dot(
+            perm_ref[...], srt_sc[...], preferred_element_type=f32
+        ).astype(bf16)
+
+
+def attend(q, text, vis, qpos, kp, perm):
+    sources, tokens, size = text.shape[0], q.shape[0], kp.shape[1]
+    ranks = size // sources
+    texts, sights = sources * tokens // size, vis.shape[0] * vis.shape[1] // size
+    blocks = texts + sights
+    tile = 32
+    rows = GROUP * tile
+    d = HEAD_DIM
+    vm = pl.BlockSpec(memory_space=pltpu.VMEM)
+    hbm = pl.BlockSpec(memory_space=pl.ANY)
+    f32, bf16 = jnp.float32, jnp.bfloat16
     return pl.pallas_call(
-        functools.partial(attend_kernel,TQ=TQ,NT=NT,NV=NV),
-        in_specs=[vm(),hb(),hb(),vm(),vm(),vm()],
-        out_specs=vm(),
-        out_shape=jax.ShapeDtypeStruct((128,2048),jnp.bfloat16),
-        scratch_shapes=[pltpu.VMEM((2,NT+NV,S,RB,D),jnp.bfloat16),pltpu.VMEM((2,NT+NV,S,RB,D),jnp.bfloat16),
-          pltpu.VMEM((2,R,KB),jnp.float32),pltpu.VMEM((2,R,128),jnp.float32),pltpu.VMEM((2,R,KB),jnp.bfloat16),pltpu.VMEM((2,R,128),jnp.float32),
-          pltpu.VMEM((R,128),jnp.float32),pltpu.VMEM((R,128),jnp.float32),pltpu.VMEM((R,128),jnp.float32),pltpu.VMEM((128,1024),jnp.bfloat16),
-          pltpu.SemaphoreType.DMA((2,NT+NV))],
-        compiler_params=pltpu.CompilerParams(vmem_limit_bytes=60<<20),
+        functools.partial(attend_kernel, tile=tile, texts=texts, sights=sights),
+        in_specs=[vm, hbm, hbm, vm, vm, vm],
+        out_specs=vm,
+        out_shape=jax.ShapeDtypeStruct(q.shape, bf16),
+        scratch_shapes=[
+            pltpu.VMEM((2, blocks + 1, sources, ranks, 2 * d), bf16), pltpu.VMEM((2, blocks, sources, ranks, 2 * d), bf16),
+            pltpu.VMEM((2, rows, size), f32), pltpu.VMEM((2, rows, d), f32), pltpu.VMEM((2, rows, size), bf16),
+            pltpu.VMEM((2, rows, 2 * d), f32), pltpu.VMEM((rows, 2 * d), f32), pltpu.VMEM((rows, d), f32),
+            pltpu.VMEM((tokens, GROUP * d), bf16), pltpu.SemaphoreType.DMA((2, 2, blocks)),
+        ],
+        compiler_params=pltpu.CompilerParams(vmem_limit_bytes=60 << 20),
         name="attend",
-    )(q,kvt,kvv4,qpos,kp,perm)
-
-
-def ring_plan(na, nb):
+    )(q, text, vis.reshape(sights, sources, ranks, vis.shape[2]), qpos, kp, perm)
+
+
+def ring_plan(na, nb, jumps=None):
     free = {}
     heap = []
     count = [0]
@@ -151,8 +199,13 @@
         if part is not None:
             na_, nb_ = (a + way, b) if axis == "a" else (a, b + way)
             send(axis, way, na_, nb_, part, at)
-    for way in (1, -1):
+    def jump(a, at):
+        for step in jumps.get(a, ()):
+            send("a", 1 if step > 0 else -1, a + step, 0, 0, at + 0.3 * (abs(step) - 1))
+    for way in () if jumps else (1, -1):
         go("a", na, way, 0, 0.0, 0, 0)
+    if jumps:
+        jump(0, 0.0)
     for way in (1, -1):
         go("b", nb, way, 0, 0.0, 0, 0)
     order = []
@@ -161,7 +214,11 @@
         at, _, axis, way, a, b, part = heapq.heappop(heap)
         order.append((axis, way, a, b, part))
         if axis == "a":
-            if part == 0:
+            if jumps:
+                jump(a, at)
+                for w in (1, -1):
+                    go("b", nb, w, 0, at, a, b)
+            elif part == 0:
                 go("a", na, way, abs(a), at, a, b)
                 for w in (1, -1):
                     go("b", nb, w, 0, at, a, b)
@@ -193,14 +250,20 @@
     ]
 
 
+JUMPS = {0: (2, -2, 1, -1), 2: (2, 1), -2: (-1,)}
+PUMPS = (1, 1, 1, 2)
+
+
 class Gather:
-    def __init__(self, own, out, cut, send_sem, recv_sem, place, core):
+    def __init__(self, own, out, cut, send_sem, recv_sem, place, core, jumps=None):
         self.own, self.out, self.rows, self.cut = own, out, own.shape[0], cut
         self.send_sem, self.recv_sem = send_sem, recv_sem
         self.y, self.z, self.ny, self.nz = place
         self.core = core
-        self.sizes = (self.nz, self.ny) if core == 0 else (self.ny, self.nz)
-        self.plan = ring_plan(*self.sizes)
+        self.along_z = core == 0 or jumps is not None
+        self.sizes = (self.nz, self.ny) if self.along_z else (self.ny, self.nz)
+        self.jumps = jumps
+        self.plan = ring_plan(*self.sizes, jumps)
         self.sent = []
         self.halves = {}
         self.next = 0
@@ -211,7 +274,7 @@
         return (y * self.nz + z) * 2 + core
 
     def source(self, a, b):
-        return self.shard(0, a, b) if self.core == 0 else self.shard(1, b, a)
+        return self.shard(self.core, a, b) if self.along_z else self.shard(self.core, b, a)
 
     def piece(self, ref, part):
         if part == 0:
@@ -229,7 +292,7 @@
         )
 
     def neighbour(self, axis, way):
-        if (axis == "a") == (self.core == 0):
+        if (axis == "a") == self.along_z:
             return {"seq_1": lax.rem(self.z + way + self.nz, self.nz)}
         return {"seq_0": lax.rem(self.y + way + self.ny, self.ny)}
 
@@ -242,9 +305,10 @@
 
     def begin(self):
         index = self.source(0, 0)
-        for axis in ("a", "b"):
-            for way in (1, -1):
-                self.send(self.own, index, 0, self.neighbour(axis, way))
+        for way in self.jumps[0] if self.jumps else (1, -1):
+            self.send(self.own, index, 0, self.neighbour("a", way))
+        for way in (1, -1):
+            self.send(self.own, index, 0, self.neighbour("b", way))
         self.send(self.own, index, 0, self.partner())
 
     def wait(self, index, part):
@@ -257,7 +321,10 @@
         size = self.sizes[0] if axis == "a" else self.sizes[1]
         off = abs(a) if axis == "a" else abs(b)
         done = True
-        if part == 0:
+        if axis == "a" and self.jumps:
+            for jump in self.jumps.get(a, ()):
+                self.send(src, index, 0, self.neighbour("a", jump))
+        elif part == 0:
             half = 0 if off + 1 < size // 2 else (1 if way == 1 else 2)
             self.send(src, index, half, self.neighbour(axis, way))
         else:
@@ -318,7 +385,7 @@
     text_loc.start()
     place = (y, z, ny, nz)
     texts = [Gather(text_ref, text_out, 64, ts, tr, place, c) for c in (0, 1)]
-    sights = [Gather(vis_own, vis_out, vis_own.shape[0] // 2, vs, vr, place, c) for c in (0, 1)]
+    sights = [Gather(vis_own, vis_out, vis_own.shape[0] // 2, vs, vr, place, c, JUMPS if nz == 8 else None) for c in (0, 1)]
 
     def on_core(act):
         for c in (0, 1):
@@ -327,7 +394,8 @@
     def pump(count):
         on_core(lambda c: texts[c].advance(count))
 
-    barrier(near(y, z, core, ny, nz) + [after, before, far])
+    skips = [{"seq_1": lax.rem(z + jump + nz, nz)} for jump in (2, -2)] if nz == 8 else []
+    barrier(near(y, z, core, ny, nz) + skips + [after, before, far])
     chunk = rows // 4
     for r in range(0, rows, chunk):
         x = patches_ref[r : r + chunk].astype(f32)
@@ -350,7 +418,7 @@
     loads[2].wait()
     q_sc[...] = jnp.dot(normed[...], qkv_w[0], preferred_element_type=f32).astype(bf16)
     bias = jnp.where(own_ids_ref[...] == near_ids_ref[...], 0.0, NEG)
-    pump(2)
+    pump(PUMPS[0])
     for halo in halos:
         halo.wait()
     scale = math.log2(math.e) / math.sqrt(VIT_HD)
@@ -371,7 +439,7 @@
         else:
             old = mixed[:, t0:t1] if t1 - t0 == 128 else jnp.concatenate([mixed[:, t0 : t0 + 128], o[:, 128:]], axis=1)
             mixed[:, t0:t1] = jnp.where(mine, o, old)
-        pump(2)
+        pump(PUMPS[1])
     loads[3].wait()
     halves = []
     half = rows // 2
@@ -385,9 +453,9 @@
             )
         )
         halves[-1].start()
-        pump(2)
+        pump(PUMPS[2])
     for i in (0, 1):
-        pump(4)
+        pump(PUMPS[3])
         halves[i].wait()
         for r in range(i * half, (i + 1) * half, chunk):
             summed = part_own[r : r + chunk].astype(f32) + part_far[r : r + chunk].astype(f32)
@@ -496,7 +564,7 @@
     )
     kp = jnp.concatenate([key_pos, all_vis_pos.reshape(-1, 1024), jnp.full((1, 1024), BIG, jnp.int32)], axis=0)
     places = places.astype(jnp.int32)
-    q_pos = (places[0] * 128 + places[1])[:, None]
+    q_pos = (places[0] * 128 + places[1])[None, :]
     attended = attend(q, all_text, all_vis, q_pos, kp, hot.T)
     return (attended, visual_kv)
 

time: 143 us -> 139 us (0.972); the launches traced: 140 us -> 138 us
  Pallas kernels: 120 us -> 118 us
where the time goes in v3:
time: 139 us; the launch traced here: 138 us
  Pallas kernels  118 us (85%)
  local copies, waits for them, and re-layouts  10.2 us (7%)
  other arithmetic  7.56 us (5%)
  matrix products  1.47 us (1%)
    pallas_call x1, Pallas kernels, encode(): pl.pallas_call(functools.partial(encode_kernel, ny=ny, nz=nz), in_specs=[...  76 us
    pallas_call x1, Pallas kernels, attend(): pl.pallas_call(functools.partial(attend_kernel, tile=tile, texts=texts, s...  42.2 us
    unnamed x16, local copies, waits for them, and re-layouts  6.78 us

profile of v3, /device:TPU:1, one launch (start us, length us, event | category | flops | bytes accessed | tf_op | source)
XLA Modules:
  0.0 138.3 jit_solution(2562300601435543259)
XLA Ops:
  0.7 0.8 copy.26
  1.5 0.2 reduce-window.7
  1.8 0.8 fusion.14
  2.6 0.3 convert_reduce_fusion
  2.9 0.8 copy.27.own_ids_ref
  3.7 0.6 and_select_fusion.near_ids_ref
  4.3 0.9 select_reduce_fusion.1
  5.2 0.7 convert_bitcast_fusion
  5.9 0.1 fusion.13
  6.0 0.9 copy.31
  6.9 0.2 convolution_convert_fusion.1
  7.1 0.7 fusion.1.text_ref
  7.8 5.8 %copy.32 = bf16[640,8,2,256]{3,1,2,0:T(8,128)(2,1)} copy(bf16[640,8,2,256]{3,2,1,0:T(2,128)(2,1)} %bitcast.21) | data formatting | bytes 10485760
  13.7 0.7 stack.38.norms_ref
  14.4 76.0 %encode.1 = (bf16[64,136,512]{2,1,0:T(8,128)(2,1)}, bf16[64,48,512]{2,1,0:T(8,128)(2,1)}, bf16[48,512]{1,0:T(8,128)(2,1)}) custom-call(bf16[136,512]{1,0:T(8,128)(2,1)} %fusion.1.text_ref, bf16[192,1280]{1,0:T(8,128)(2,1)} %patches_ref.1, f32[5,1280]{1,0:T(8,128)} %stack.38.norms_ref, s32[192,1]{1,0:T(8,128)} %copy.27.own_ids_ref, ...), custom_call_target="tpu_custom_call" | custom-call | tf_op jit(solution)/shard_map/encode/pallas_call | solution.py:499
  90.4 0.9 slice_convert_fusion
  91.6 0.2 reshape.91
  91.8 0.5 select_reduce_fusion
  92.4 0.7 add_add_fusion.kp_ref
  93.1 0.5 slice_add_fusion.1.qpos_ref
  93.6 1.2 convolution_convert_fusion.q_ref
  94.7 0.7 fusion.3.perm_ref
  95.4 42.2 %attend.1 = bf16[128,2048]{1,0:T(8,128)(2,1)} custom-call(bf16[128,2048]{1,0:T(8,128)(2,1)} %convolution_convert_fusion.q_ref, bf16[64,136,512]{2,1,0:T(8,128)(2,1)} %get-tuple-element.5.text_ref, bf16[3,64,16,512]{3,2,1,0:T(8,128)(2,1)} %bitcast.23, s32[1,128]{1,0:T(1,128)} %slice_add_fusion.1.qpos_ref, s32[12,1024]{1,0:T(8,128)} %add_add_fusion.kp_ref, ...), custom_call_target="tpu_custom_call" | custom-call | tf_op jit(solution)/shard_map/attend/pallas_call | solution.py:162
  137.7 0.6 reshape.92
  (31 shorter events, 0.6 us)
Async XLA Ops:
  0.6 92.9 %copy-start = (bf16[128,2048]{1,0:T(8,128)(2,1)S(1)}, bf16[128,2048]{1,0:T(8,128)(2,1)}, u32[]{:S(2)}) copy-start(bf16[128,2048]{1,0:T(8,128)(2,1)} %param.26) | copy-start | bytes 1572868
  7.8 5.8 %copy-start.2 = (f32[1280]{0:T(1024)S(1)}, f32[1280]{0:T(1024)}, u32[]{:S(2)}) copy-start(f32[1280]{0:T(1024)} %param.15) | copy-start | bytes 15364
  7.8 5.8 %copy-start.3 = (f32[1280]{0:T(1024)S(1)}, f32[1280]{0:T(1024)}, u32[]{:S(2)}) copy-start(f32[1280]{0:T(1024)} %param.16) | copy-start | bytes 15364
  7.8 5.9 %copy-start.4 = (f32[1280]{0:T(1024)S(1)}, f32[1280]{0:T(1024)}, u32[]{:S(2)}) copy-start(f32[1280]{0:T(1024)} %param.19) | copy-start | bytes 15364
  7.8 5.9 %copy-start.5 = (f32[1280]{0:T(1024)S(1)}, f32[1280]{0:T(1024)}, u32[]{:S(2)}) copy-start(f32[1280]{0:T(1024)} %param.20) | copy-start | bytes 15364
  7.8 5.9 %copy-start.6 = (f32[1280]{0:T(1024)S(1)}, f32[1280]{0:T(1024)}, u32[]{:S(2)}) copy-start(f32[1280]{0:T(1024)} %param.21) | copy-start | bytes 15364
  95.4 42.2 %copy-start.1 = (bf16[48,512]{1,0:T(8,128)(2,1)S(1)}, bf16[48,512]{1,0:T(8,128)(2,1)}, u32[]{:S(2)}) copy-start(bf16[48,512]{1,0:T(8,128)(2,1)} %get-tuple-element.7) | copy-start | bytes 147460

commit v4 on v3

--- a/solution.py
+++ b/solution.py
@@ -361,8 +361,8 @@
 def encode_kernel(
     text_ref, patches_ref, norms_ref, own_ids_ref, near_ids_ref, qkv_hbm, proj_hbm, wv_hbm,
     text_out, vis_out, vis_own,
-    qkv_w, proj_w, wv, normed, q_sc, keys, values, mixed, part_own, part_far, merged,
-    weight_sem, halo_sem, far_sem, ts, tr, vs, vr, loc_sem, *, ny, nz,
+    qkv_w, proj_w, wv, normed, q_sc, keys, values, mixed, mixed_own, mixed_far, proj_far, summed, merged,
+    weight_sem, halo_sem, far_sem, proj_sem, ts, tr, vs, vr, loc_sem, *, ny, nz,
 ):
     f32, bf16 = jnp.float32, jnp.bfloat16
     y, z, core = lax.axis_index("seq_0"), lax.axis_index("seq_1"), lax.axis_index("seq_2")
@@ -396,6 +396,18 @@
 
     skips = [{"seq_1": lax.rem(z + jump + nz, nz)} for jump in (2, -2)] if nz == 8 else []
     barrier(near(y, z, core, ny, nz) + skips + [after, before, far])
+    share = proj_hbm.shape[0] // 2
+    my_share = pl.ds(pl.multiple_of(core * share, share), share)
+
+    def hand(src, number, device):
+        return pltpu.make_async_remote_copy(
+            src_ref=src, dst_ref=proj_far.at[my_share],
+            send_sem=proj_sem.at[0, number], recv_sem=proj_sem.at[1, number], device_id=device, device_id_type=MESH,
+        )
+
+    push = hand(proj_hbm.at[my_share], 0, far)
+    push.start()
+    forward = hand(proj_far.at[my_share], 1, {"seq_2": 1 - core})
     chunk = rows // 4
     for r in range(0, rows, chunk):
         x = patches_ref[r : r + chunk].astype(f32)
@@ -422,6 +434,7 @@
     for halo in halos:
         halo.wait()
     scale = math.log2(math.e) / math.sqrt(VIT_HD)
+    tiles = []
     for h in range(cols // VIT_HD):
         lo, hi = h * VIT_HD, (h + 1) * VIT_HD
         t0, t1 = lo // 128 * 128, -(-hi // 128) * 128
@@ -439,30 +452,35 @@
         else:
             old = mixed[:, t0:t1] if t1 - t0 == 128 else jnp.concatenate([mixed[:, t0 : t0 + 128], o[:, 128:]], axis=1)
             mixed[:, t0:t1] = jnp.where(mine, o, old)
+        for t in range(len(tiles), hi // 128):
+            mixed_own[t] = mixed[:, t * 128 : (t + 1) * 128].astype(bf16)
+            tiles.append(
+                pltpu.make_async_remote_copy(
+                    src_ref=mixed_own.at[t], dst_ref=mixed_far.at[t],
+                    send_sem=far_sem.at[0, t], recv_sem=far_sem.at[1, t], device_id=far, device_id_type=MESH,
+                )
+            )
+            tiles[-1].start()
         pump(PUMPS[1])
+    push.wait()
+    forward.start()
     loads[3].wait()
-    halves = []
-    half = rows // 2
-    for i in (0, 1):
-        part = slice(i * half, (i + 1) * half)
-        part_own[part] = jnp.dot(mixed[part].astype(bf16), proj_w[...], preferred_element_type=f32).astype(bf16)
-        halves.append(
-            pltpu.make_async_remote_copy(
-                src_ref=part_own.at[part], dst_ref=part_far.at[part],
-                send_sem=far_sem.at[0, i], recv_sem=far_sem.at[1, i], device_id=far, device_id_type=MESH,
-            )
-        )
-        halves[-1].start()
-        pump(PUMPS[2])
-    for i in (0, 1):
-        pump(PUMPS[3])
-        halves[i].wait()
-        for r in range(i * half, (i + 1) * half, chunk):
-            summed = part_own[r : r + chunk].astype(f32) + part_far[r : r + chunk].astype(f32)
-            x = (patches_ref[r : r + chunk].astype(f32) + summed + norms_ref[2:3]).astype(bf16)
-            x = norm_rows(x.astype(f32), norms_ref[3:4], norms_ref[4:5])
-            for t in range(width // 128):
-                merged[t, r : r + chunk] = x[:, t * 128 : (t + 1) * 128]
+
+    def projected(parts, weight):
+        return jnp.dot(jnp.concatenate([parts[t] for t in range(cols // 128)], axis=1), weight[...], preferred_element_type=f32)
+
+    summed[...] = projected(mixed_own, proj_w)
+    pump(PUMPS[2])
+    forward.wait()
+    for tile in tiles:
+        tile.wait()
+    summed[...] = summed[...] + projected(mixed_far, proj_far)
+    for r in range(0, rows, chunk):
+        x = (patches_ref[r : r + chunk].astype(f32) + summed[r : r + chunk] + norms_ref[2:3]).astype(bf16)
+        x = norm_rows(x.astype(f32), norms_ref[3:4], norms_ref[4:5])
+        for t in range(width // 128):
+            merged[t, r : r + chunk] = x[:, t * 128 : (t + 1) * 128]
+    pump(PUMPS[3])
     loads[4].wait()
     tokens = rows // 4
     total = jnp.zeros((tokens, wv.shape[1]), f32)
@@ -509,9 +527,10 @@
             pltpu.VMEM(qkv.shape, bf16), pltpu.VMEM(proj.shape, bf16), pltpu.VMEM(wv.shape, bf16),
             pltpu.VMEM((rows, width), bf16), pltpu.VMEM((rows, cols), bf16),
             pltpu.VMEM((3, rows, cols), bf16), pltpu.VMEM((3, rows, cols), bf16),
-            pltpu.VMEM((rows, cols), f32), pltpu.VMEM((rows, width), bf16), pltpu.VMEM((rows, width), bf16),
+            pltpu.VMEM((rows, cols), f32), pltpu.VMEM((cols // 128, rows, 128), bf16),
+            pltpu.VMEM((cols // 128, rows, 128), bf16), pltpu.VMEM(proj.shape, bf16), pltpu.VMEM((rows, width), f32),
             pltpu.VMEM((width // 128, rows, 128), f32),
-            dma((5,)), dma((2, 4)), dma((2, 2)),
+            dma((5,)), dma((2, 4)), dma((2, cols // 128)), dma((2, 2)),
             dma((2 * n + 16,)), dma((n, 2)), dma((2 * n + 16,)), dma((n, 2)), dma((2,)),
         ],
         compiler_params=pltpu.CompilerParams(collective_id=1, has_side_effects=True, vmem_limit_bytes=60 << 20),

time: 139 us -> 134 us (0.964)
  Pallas kernels: 118 us -> 114 us
    pallas_call x1, Pallas kernels: 76 us -> 71.7 us  [encode(): pl.pallas_call(functools.partial(encode_kernel, ny=ny, nz=nz), in_specs=[...]
where the time goes in v4:
time: 134 us
  Pallas kernels  114 us (85%)
  local copies, waits for them, and re-layouts  10.2 us (8%)
  other arithmetic  7.56 us (6%)
  matrix products  1.47 us (1%)
    pallas_call x1, Pallas kernels, encode(): pl.pallas_call(functools.partial(encode_kernel, ny=ny, nz=nz), in_specs=[...  71.7 us
    pallas_call x1, Pallas kernels, attend(): pl.pallas_call(functools.partial(attend_kernel, tile=tile, texts=texts, s...  42.2 us
    unnamed x16, local copies, waits for them, and re-layouts  6.78 us

profile of v4, /device:TPU:1, one launch (start us, length us, event | category | flops | bytes accessed | tf_op | source)
XLA Modules:
  0.0 134.1 jit_solution(4820441281624583733)
XLA Ops:
  0.7 0.8 copy.26
  1.5 0.2 reduce-window.7
  1.8 0.8 fusion.14
  2.6 0.3 convert_reduce_fusion
  2.9 0.8 copy.27.own_ids_ref
  3.7 0.6 and_select_fusion.near_ids_ref
  4.3 0.9 select_reduce_fusion.1
  5.2 0.7 convert_bitcast_fusion
  5.9 0.1 fusion.13
  6.0 0.9 copy.31
  6.9 0.2 convolution_convert_fusion.1
  7.1 0.7 fusion.1.text_ref
  7.8 5.8 %copy.32 = bf16[640,8,2,256]{3,1,2,0:T(8,128)(2,1)} copy(bf16[640,8,2,256]{3,2,1,0:T(2,128)(2,1)} %bitcast.21) | data formatting | bytes 10485760
  13.7 0.7 stack.38.norms_ref
  14.4 71.7 %encode.1 = (bf16[64,136,512]{2,1,0:T(8,128)(2,1)}, bf16[64,48,512]{2,1,0:T(8,128)(2,1)}, bf16[48,512]{1,0:T(8,128)(2,1)}) custom-call(bf16[136,512]{1,0:T(8,128)(2,1)} %fusion.1.text_ref, bf16[192,1280]{1,0:T(8,128)(2,1)} %patches_ref.1, f32[5,1280]{1,0:T(8,128)} %stack.38.norms_ref, s32[192,1]{1,0:T(8,128)} %copy.27.own_ids_ref, ...), custom_call_target="tpu_custom_call" | custom-call | tf_op jit(solution)/shard_map/encode/pallas_call | solution.py:517
  86.1 0.9 slice_convert_fusion
  87.4 0.2 reshape.91
  87.5 0.5 select_reduce_fusion
  88.1 0.7 add_add_fusion.kp_ref
  88.8 0.5 slice_add_fusion.1.qpos_ref
  89.3 1.2 convolution_convert_fusion.q_ref
  90.5 0.7 fusion.3.perm_ref
  91.2 42.2 %attend.1 = bf16[128,2048]{1,0:T(8,128)(2,1)} custom-call(bf16[128,2048]{1,0:T(8,128)(2,1)} %convolution_convert_fusion.q_ref, bf16[64,136,512]{2,1,0:T(8,128)(2,1)} %get-tuple-element.5.text_ref, bf16[3,64,16,512]{3,2,1,0:T(8,128)(2,1)} %bitcast.23, s32[1,128]{1,0:T(1,128)} %slice_add_fusion.1.qpos_ref, s32[12,1024]{1,0:T(8,128)} %add_add_fusion.kp_ref, ...), custom_call_target="tpu_custom_call" | custom-call | tf_op jit(solution)/shard_map/attend/pallas_call | solution.py:162
  133.4 0.6 reshape.92
  (31 shorter events, 0.6 us)
Async XLA Ops:
  0.6 88.7 %copy-start = (bf16[128,2048]{1,0:T(8,128)(2,1)S(1)}, bf16[128,2048]{1,0:T(8,128)(2,1)}, u32[]{:S(2)}) copy-start(bf16[128,2048]{1,0:T(8,128)(2,1)} %param.26) | copy-start | bytes 1572868
  7.8 5.8 %copy-start.2 = (f32[1280]{0:T(1024)S(1)}, f32[1280]{0:T(1024)}, u32[]{:S(2)}) copy-start(f32[1280]{0:T(1024)} %param.15) | copy-start | bytes 15364
  7.8 5.8 %copy-start.3 = (f32[1280]{0:T(1024)S(1)}, f32[1280]{0:T(1024)}, u32[]{:S(2)}) copy-start(f32[1280]{0:T(1024)} %param.16) | copy-start | bytes 15364
  7.8 5.9 %copy-start.4 = (f32[1280]{0:T(1024)S(1)}, f32[1280]{0:T(1024)}, u32[]{:S(2)}) copy-start(f32[1280]{0:T(1024)} %param.19) | copy-start | bytes 15364
  7.8 5.9 %copy-start.5 = (f32[1280]{0:T(1024)S(1)}, f32[1280]{0:T(1024)}, u32[]{:S(2)}) copy-start(f32[1280]{0:T(1024)} %param.20) | copy-start | bytes 15364
  7.8 5.9 %copy-start.6 = (f32[1280]{0:T(1024)S(1)}, f32[1280]{0:T(1024)}, u32[]{:S(2)}) copy-start(f32[1280]{0:T(1024)} %param.21) | copy-start | bytes 15364
  91.2 42.2 %copy-start.1 = (bf16[48,512]{1,0:T(8,128)(2,1)S(1)}, bf16[48,512]{1,0:T(8,128)(2,1)}, u32[]{:S(2)}) copy-start(bf16[48,512]{1,0:T(8,128)(2,1)} %get-tuple-element.7) | copy-start | bytes 147460
